TPU v7x, 512 devices: a whole 4x8x8 slice. The times are simulated.
512 devices in a mesh: section: 8 (over y_hi, core), expert: 8 (over x, y_lo), tensor: 8 (over z).
Axes of the slice: x: 4, y: 8 (y_hi: 4, y_lo: 2; y = y_hi * 2 + y_lo), z: 8, core: 2. Of those that a mesh axis runs over, the one named last changes fastest.
Arguments:
- branch_weights: bfloat16 [8, 8192, 8192], P('expert', ('section', 'tensor')), may hold values from -0.125 to 0.125
- branch_gains: float32 [8, 8192], P('expert', ('section', 'tensor')), may hold values from 0.1 to 1.9
- column_order: int32 [8, 8192], P('expert'), may hold values from 0 to 8191, each once within a row
- layer_order: int32 [4], replicated, may hold values from 0 to 3, each once
- probe_seeds: int32 [1024], replicated, may hold values from 1 to 32767
Outputs:
- expert_weights: bfloat16 [8, 8192, 8192], P('expert', None, ('section', 'tensor'))
- checksum: float32 [8, 1024, 8192], P('expert', None, ('section', 'tensor'))
- fingerprint: float32 [8, 1024], P('expert')
- shared_gain: float32 [8192], replicated
Inputs may be any that keep to these rules, and one draw needn't show every extreme that they name: Each row of column_order names every hidden unit once. layer_order names every layer once.
All inputs are finite; a program needn't handle non-finite values.
Results may differ from a plain program's by a relative error of at most 0.0034.
Values may be sent and summed in bfloat16 or wider, within the bound.
No kernel may reach another device: no remote copies, remote signals or barrier semaphores. Data moves between devices by JAX's collectives and lax.ppermute only.
A program may use at most 64 MiB of HBM per device.

v0:
```python
import jax
import jax.numpy as jnp
from jax import lax
from jax.sharding import PartitionSpec as P

D = 2048
FF = 8192


def from_everyone(value, axis):
    length = lax.axis_size(axis)
    return lax.all_to_all(
        jnp.broadcast_to(value[None], (length, *value.shape)), axis, 0, 0, tiled=True
    )


def taken_together(value, axis):
    everything = from_everyone(value, axis)
    return jnp.sum(everything, axis=0)


def laid_out(tiles, dim):
    shape = list(tiles.shape[1:])
    shape[dim] *= tiles.shape[0]
    return jnp.moveaxis(tiles, 0, dim).reshape(shape)


def gather_directly(value, axis, dim):
    tiles = from_everyone(value, axis)
    return laid_out(tiles, dim)


def probe_at(probe_seeds, row_ids):
    hashed = probe_seeds[:, None] * (row_ids[None, :] + 1) % 65521
    return (hashed % 511 - 255).astype(jnp.float32) / 256.0


def sketch(natural, probe_seeds):
    segment_rows = D // 2
    running = jnp.zeros((probe_seeds.shape[0], natural.shape[1]), jnp.float32)
    for portion in range(natural.shape[0] // segment_rows):
        row_ids = portion * segment_rows + lax.iota(jnp.int32, segment_rows)
        probes = probe_at(probe_seeds, row_ids).astype(jnp.bfloat16)
        running = running + jnp.dot(
            probes,
            natural[portion * segment_rows : (portion + 1) * segment_rows],
            preferred_element_type=jnp.float32,
        )
    return running


def local(branch_weights, branch_gains, column_order, layer_order, probe_seeds):
    weights = branch_weights[0]
    rows_dev = weights.shape[0]
    n_section = lax.axis_size("section")
    n_tensor = lax.axis_size("tensor")
    groups = n_section * n_tensor
    cols_dev = weights.shape[1] // groups
    layers = layer_order.shape[0]
    own_gains = branch_gains[0]
    mean_gains = taken_together(own_gains, "expert") / lax.axis_size("expert")
    scaling = own_gains / mean_gains
    permuted = jnp.take(weights, column_order[0], axis=1)
    folded = (permuted.astype(jnp.float32) * scaling[:, None]).astype(jnp.bfloat16)
    per_layer = D // rows_dev
    slot_ids = lax.iota(jnp.int32, layers)
    inverse = jnp.sum(
        jnp.where(layer_order[None, :] == slot_ids[:, None], slot_ids[None, :], 0), axis=1
    )
    block_ids = lax.iota(jnp.int32, groups)
    layer_ids = block_ids // per_layer
    source_pos = (
        jnp.sum(jnp.where(layer_ids[:, None] == slot_ids[None, :], inverse[None, :], 0), axis=1)
        * per_layer
        + block_ids % per_layer
    )
    all_gains = gather_directly(mean_gains, ("section", "tensor"), 0)
    shared_gain = all_gains.reshape(groups, rows_dev)[source_pos].reshape(groups * rows_dev)
    device = lax.axis_index(("section", "tensor"))
    seven = jnp.full((1,), 7919, jnp.int32)
    arrived = lax.all_to_all(
        folded.reshape(rows_dev, groups, cols_dev),
        ("section", "tensor"),
        split_axis=1,
        concat_axis=0,
        tiled=True,
    )
    width_cols = arrived.shape[2]
    ordered = arrived.reshape(groups, rows_dev, width_cols)[source_pos].reshape(
        groups * rows_dev, width_cols
    )
    sketches = sketch(ordered, probe_seeds)
    column_probe = probe_at(seven, device * cols_dev + lax.iota(jnp.int32, cols_dev))[0]
    partial_print = jnp.dot(sketches, column_probe, precision=lax.Precision.HIGHEST)
    fingerprint = taken_together(partial_print, ("section", "tensor")) * FF ** (-0.5)
    return (ordered[None], sketches[None], fingerprint[None], shared_gain)


def solution(mesh):
    return jax.shard_map(
        local,
        mesh=mesh,
        in_specs=(
            P("expert", ("section", "tensor"), None),
            P("expert", ("section", "tensor")),
            P("expert", None),
            P(),
            P(),
        ),
        out_specs=(
            P("expert", None, ("section", "tensor")),
            P("expert", None, ("section", "tensor")),
            P("expert", None),
            P(),
        ),
        check_vma=False,
    )
```

profile of v0, /device:TPU:8, one launch (start us, length us, event | category | flops | bytes accessed | tf_op | source)
XLA Modules:
  0.0 205.2 jit_solution(12573902976384038236)
XLA Ops:
  0.6 1.3 broadcast_in_dim.44
  1.9 9.0 %all-to-all-start = ((f32[8,1,128]{2,1,0:T(1,128)}), f32[8,1,128]{2,1,0:T(1,128)S(1)}, u32[]{:S(2)}, u32[]{:S(2)}) async-start(f32[8,1,128]{2,1,0:T(1,128)} %broadcast_in_dim.44), calls=%async_computation | async-start | bytes 8192 | tf_op jit(solution)/shard_map/all_to_all | solution.py:12
  10.9 0.8 compare_select_fusion
  11.7 0.8 compare_and_fusion
  12.5 3.2 %copy.18 = bf16[1,128,8192]{1,2,0:T(8,128)(2,1)S(1)} copy(bf16[1,128,8192]{2,1,0:T(8,128)(2,1)} %param.5) | data formatting | bytes 4194304 | tf_op args[0]
  15.7 29.5 %gather_fusion = bf16[8192,128]{1,0:T(8,128)(2,1)} fusion(bf16[128,8192]{0,1:T(8,128)(2,1)S(1)} %bitcast.48, s32[8192]{0:T(1024)S(1)} %broadcast_clamp_fusion), kind=kCustom, calls=%fused_computation | custom fusion | bytes 4227072 | tf_op jit(solution)/shard_map/jit(_take)/gather | solution.py:63
  45.2 0.0 copy-start.3
  45.2 3.2 %copy.19 = bf16[128,64,128]{2,0,1:T(8,128)(2,1)S(1)} copy(bf16[128,64,128]{0,2,1:T(8,128)(2,1)} %bitcast.49) | data formatting | bytes 4194304 | tf_op jit(solution)/shard_map/jit(_take)/gather | solution.py:63
  48.5 0.0 all-to-all-done
  48.5 0.0 copy-done.3
  48.5 2.1 %multiply_convert_fusion = bf16[128,64,128]{2,0,1:T(8,128)(2,1)} fusion(f32[128]{0:T(128)S(1)} %get-tuple-element.13, bf16[128,64,128]{2,0,1:T(8,128)(2,1)S(1)} %copy.19, pred[64,128]{1,0:T(8,128)(4,1)S(1)} %compare_and_fusion), kind=kLoop, calls=%fused_computation.99 | loop fusion | flops 4194304 | bytes 4203008 | tf_op jit(solution)/shard_map/convert_element_type | solution.py:64
  50.7 0.0 copy-start.5
  50.7 12.5 %all-to-all-start.1 = ((bf16[128,64,128]{2,0,1:T(8,128)(2,1)}), bf16[128,64,128]{2,0,1:T(8,128)(2,1)S(1)}, u32[]{:S(2)}, u32[]{:S(2)}) async-start(bf16[128,64,128]{2,0,1:T(8,128)(2,1)} %multiply_convert_fusion), calls=%async_computation.1 | async-start | bytes 4194304 | tf_op jit(solution)/shard_map/all_to_all | solution.py:81
  63.3 0.0 copy-done.5
  63.3 0.1 select_reduce_fusion.1
  63.4 0.1 select_reduce_fusion
  63.5 53.0 %all-to-all-done.1 = bf16[128,64,128]{2,0,1:T(8,128)(2,1)S(1)} async-done(((bf16[128,64,128]{2,0,1:T(8,128)(2,1)}), bf16[128,64,128]{2,0,1:T(8,128)(2,1)S(1)}, u32[]{:S(2)}, u32[]{:S(2)}) %all-to-all-start.1) | async-done | bytes 2097184 | tf_op jit(solution)/shard_map/all_to_all | solution.py:81
  116.5 0.0 copy-start.1
  116.5 0.7 broadcast_in_dim.51
  117.2 11.4 %all-to-all-start.3 = ((f32[64,1,128]{2,1,0:T(1,128)}), f32[64,1,128]{2,1,0:T(1,128)S(1)}, u32[]{:S(2)}, u32[]{:S(2)}) async-start(f32[64,1,128]{2,1,0:T(1,128)} %broadcast_in_dim.51), calls=%async_computation.3 | async-start | bytes 65536 | tf_op jit(solution)/shard_map/all_to_all | solution.py:12
  128.6 0.0 copy-done.1
  128.6 2.5 %gather_fusion.1 = bf16[64,128,128]{2,1,0:T(8,128)(2,1)S(1)} fusion(bf16[64,128,128]{2,1,0:T(8,128)(2,1)} %bitcast.51, s32[1024]{0:T(1024)S(1)} %pad_clamp_fusion), kind=kCustom, calls=%fused_computation.1 | custom fusion | bytes 4194560 | tf_op jit(solution)/shard_map/gather | solution.py:89
  131.2 0.0 copy-start
  131.2 0.0 copy-start.4
  131.2 0.2 fusion.194
  131.4 1.1 copy-done
  132.5 0.0 copy-done.4
  132.5 5.2 %fusion.100 = f32[1024,128]{1,0:T(8,128)S(1)} fusion(bf16[1024,128]{1,0:T(8,128)(2,1)S(1)} %bitcast.61, s32[1024]{0:T(1024)S(1)} %iota_add_fusion.6, s32[1024]{0:T(1024)S(1)} %copy-done.4), kind=kOutput, calls=%fused_computation.122 | convolution fusion | flops 286261248 | bytes 794624 | tf_op jit(solution)/shard_map/dot_general | solution.py:44
  137.7 5.3 %fusion.104 = f32[1024,128]{1,0:T(8,128)S(1)} fusion(f32[1024,128]{1,0:T(8,128)S(1)} %fusion.100, bf16[1024,128]{1,0:T(8,128)(2,1)S(1)} %bitcast.60, s32[1024]{0:T(1024)S(1)} %iota_add_fusion.7, s32[1024]{0:T(1024)S(1)} %copy-done.4), kind=kOutput, calls=%fused_computation.124 | convolution fusion | flops 286392320 | bytes 1318912 | tf_op jit(solution)/shard_map/dot_general | solution.py:44
  143.0 5.5 %fusion.107 = f32[1024,128]{1,0:T(8,128)S(1)} fusion(f32[1024,128]{1,0:T(8,128)S(1)} %fusion.104, bf16[1024,128]{1,0:T(8,128)(2,1)S(1)} %bitcast.59, s32[1024]{0:T(1024)S(1)} %iota_add_fusion.5, s32[1024]{0:T(1024)S(1)} %copy-done.4), kind=kOutput, calls=%fused_computation.125 | convolution fusion | flops 286392320 | bytes 1318912 | tf_op jit(solution)/shard_map/dot_general | solution.py:44
  148.5 5.3 %fusion.110 = f32[1024,128]{1,0:T(8,128)S(1)} fusion(f32[1024,128]{1,0:T(8,128)S(1)} %fusion.107, bf16[1024,128]{1,0:T(8,128)(2,1)S(1)} %bitcast.58, s32[1024]{0:T(1024)S(1)} %iota_add_fusion.4, s32[1024]{0:T(1024)S(1)} %copy-done.4), kind=kOutput, calls=%fused_computation.126 | convolution fusion | flops 286392320 | bytes 1318912 | tf_op jit(solution)/shard_map/dot_general | solution.py:44
  153.8 5.5 %fusion.113 = f32[1024,128]{1,0:T(8,128)S(1)} fusion(f32[1024,128]{1,0:T(8,128)S(1)} %fusion.110, bf16[1024,128]{1,0:T(8,128)(2,1)S(1)} %bitcast.57, s32[1024]{0:T(1024)S(1)} %iota_add_fusion.3, s32[1024]{0:T(1024)S(1)} %copy-done.4), kind=kOutput, calls=%fused_computation.127 | convolution fusion | flops 286392320 | bytes 1318912 | tf_op jit(solution)/shard_map/dot_general | solution.py:44
  159.3 5.3 %fusion.116 = f32[1024,128]{1,0:T(8,128)S(1)} fusion(f32[1024,128]{1,0:T(8,128)S(1)} %fusion.113, bf16[1024,128]{1,0:T(8,128)(2,1)S(1)} %bitcast.56, s32[1024]{0:T(1024)S(1)} %iota_add_fusion.2, s32[1024]{0:T(1024)S(1)} %copy-done.4), kind=kOutput, calls=%fused_computation.128 | convolution fusion | flops 286392320 | bytes 1318912 | tf_op jit(solution)/shard_map/dot_general | solution.py:44
  164.7 5.6 %fusion.119 = f32[1024,128]{1,0:T(8,128)S(1)} fusion(f32[1024,128]{1,0:T(8,128)S(1)} %fusion.116, bf16[1024,128]{1,0:T(8,128)(2,1)S(1)} %bitcast.55, s32[1024]{0:T(1024)S(1)} %iota_add_fusion.1, s32[1024]{0:T(1024)S(1)} %copy-done.4), kind=kOutput, calls=%fused_computation.129 | convolution fusion | flops 286392320 | bytes 1318912 | tf_op jit(solution)/shard_map/dot_general | solution.py:44
  170.2 5.3 %fusion.122 = f32[1024,128]{1,0:T(8,128)S(1)} fusion(f32[1024,128]{1,0:T(8,128)S(1)} %fusion.119, bf16[1024,128]{1,0:T(8,128)(2,1)S(1)} %bitcast.54, s32[1024]{0:T(1024)S(1)} %iota_add_fusion, s32[1024]{0:T(1024)S(1)} %copy-done.4), kind=kOutput, calls=%fused_computation.130 | convolution fusion | flops 286392320 | bytes 1318912 | tf_op jit(solution)/shard_map/dot_general | solution.py:44
  175.5 0.0 copy-start.2
  175.5 0.5 fusion.131
  176.0 0.0 all-to-all-done.3
  176.0 0.9 broadcast_in_dim.50
  176.9 12.7 %all-to-all-start.2 = ((f32[64,1,1024]{2,1,0:T(1,128)}), f32[64,1,1024]{2,1,0:T(1,128)S(1)}, u32[]{:S(2)}, u32[]{:S(2)}) async-start(f32[64,1,1024]{2,1,0:T(1,128)} %broadcast_in_dim.50), calls=%async_computation.2 | async-start | bytes 524288 | tf_op jit(solution)/shard_map/all_to_all | solution.py:12
  189.6 1.2 gather_fusion.2
  190.8 13.2 %all-to-all-done.2 = f32[64,1,1024]{2,1,0:T(1,128)S(1)} async-done(((f32[64,1,1024]{2,1,0:T(1,128)}), f32[64,1,1024]{2,1,0:T(1,128)S(1)}, u32[]{:S(2)}, u32[]{:S(2)}) %all-to-all-start.2) | async-done | bytes 262176 | tf_op jit(solution)/shard_map/all_to_all | solution.py:12
  204.0 0.2 reduce_sum.39
  204.1 0.6 broadcast_multiply_fusion
  204.7 0.0 copy-done.2
  (14 shorter events, 0.1 us)
Async XLA Ops:
  1.9 46.6 %all-to-all-start = ((f32[8,1,128]{2,1,0:T(1,128)}), f32[8,1,128]{2,1,0:T(1,128)S(1)}, u32[]{:S(2)}, u32[]{:S(2)}) async-start(f32[8,1,128]{2,1,0:T(1,128)} %broadcast_in_dim.44), calls=%async_computation | async-start | bytes 8192 | tf_op jit(solution)/shard_map/all_to_all | solution.py:12
  45.2 3.3 %copy-start.3 = (f32[1,128]{1,0:T(1,128)S(1)}, f32[1,128]{1,0:T(1,128)}, u32[]{:S(2)}) copy-start(f32[1,128]{1,0:T(1,128)} %param.6) | copy-start | bytes 1540
  50.7 12.7 %copy-start.5 = (s32[4]{0:T(128)S(1)}, s32[4]{0:T(128)}, u32[]{:S(2)}) copy-start(s32[4]{0:T(128)} %param.8) | copy-start | bytes 52
  50.7 65.9 %all-to-all-start.1 = ((bf16[128,64,128]{2,0,1:T(8,128)(2,1)}), bf16[128,64,128]{2,0,1:T(8,128)(2,1)S(1)}, u32[]{:S(2)}, u32[]{:S(2)}) async-start(bf16[128,64,128]{2,0,1:T(8,128)(2,1)} %multiply_convert_fusion), calls=%async_computation.1 | async-start | bytes 4194304 | tf_op jit(solution)/shard_map/all_to_all | solution.py:81
  116.5 12.1 %copy-start.1 = (bf16[128,64,128]{2,0,1:T(8,128)(2,1)}, bf16[128,64,128]{2,0,1:T(8,128)(2,1)S(1)}, u32[]{:S(2)}) copy-start(bf16[128,64,128]{2,0,1:T(8,128)(2,1)S(1)} %all-to-all-done.1) | copy-start | bytes 6291460
  117.2 58.8 %all-to-all-start.3 = ((f32[64,1,128]{2,1,0:T(1,128)}), f32[64,1,128]{2,1,0:T(1,128)S(1)}, u32[]{:S(2)}, u32[]{:S(2)}) async-start(f32[64,1,128]{2,1,0:T(1,128)} %broadcast_in_dim.51), calls=%async_computation.3 | async-start | bytes 65536 | tf_op jit(solution)/shard_map/all_to_all | solution.py:12
  131.2 1.3 copy-start
  131.2 1.3 copy-start.4
  175.5 29.3 %copy-start.2 = (f32[1024,128]{1,0:T(8,128)}, f32[1024,128]{1,0:T(8,128)S(1)}, u32[]{:S(2)}) copy-start(f32[1024,128]{1,0:T(8,128)S(1)} %fusion.122) | copy-start | bytes 1572868
  176.9 27.1 %all-to-all-start.2 = ((f32[64,1,1024]{2,1,0:T(1,128)}), f32[64,1,1024]{2,1,0:T(1,128)S(1)}, u32[]{:S(2)}, u32[]{:S(2)}) async-start(f32[64,1,1024]{2,1,0:T(1,128)} %broadcast_in_dim.50), calls=%async_computation.2 | async-start | bytes 524288 | tf_op jit(solution)/shard_map/all_to_all | solution.py:12
where the time goes:
time: 209 us; the launch traced here: 205 us
  waiting for transfers between devices  66.1 us (32%)
  starting transfers between devices  45.7 us (22%)
  local copies, waits for them, and re-layouts  43.8 us (21%)
  matrix products  43.5 us (21%)
  other arithmetic  4.78 us (2%)
    all_to_all x1, waiting for transfers between devices, local(): lax.all_to_all(folded.reshape(rows_dev, groups, cols_dev), ('section', 't...  53 us
    dot_general x8, matrix products, sketch(): jnp.dot(probes, natural[portion * segment_rows:(portion + 1) * segment_ro...  43 us
    all_to_all x3, starting transfers between devices, from_everyone(): lax.all_to_all(jnp.broadcast_to(value[None], (length, *value.shape)), axi...  33.1 us
    gather x2, local copies, waits for them, and re-layouts, local(): permuted = jnp.take(weights, column_order[0], axis=1)  32.7 us
    all_to_all x3, waiting for transfers between devices, from_everyone(): lax.all_to_all(jnp.broadcast_to(value[None], (length, *value.shape)), axi...  13.2 us
    all_to_all x1, starting transfers between devices, local(): lax.all_to_all(folded.reshape(rows_dev, groups, cols_dev), ('section', 't...  12.5 us
    unnamed x13, local copies, waits for them, and re-layouts  4.3 us
  transfers between devices with their start and end apart: 4, of which 2 were waited for; matrix products, arithmetic and copies ran while one was open for 42% of the time, Pallas kernels for 0%

commit v1 on v0

v1 whole, which is shorter than its diff:
```python
import functools

import jax
import jax.numpy as jnp
import numpy as np
from jax import lax
from jax.experimental import pallas as pl
from jax.experimental.pallas import tpu as pltpu
from jax.sharding import PartitionSpec as P

D = 2048
FF = 8192
LAYERS = 4
PROBES = 1024
ROWS = 128
COLS = 128
GROUPS = 64
SENT = ROWS + 8
PRIME = 65521
STACK = ("section", "tensor")
MIB = 1 << 20

VMEM = pl.BlockSpec(memory_space=pltpu.VMEM)
SMEM = pl.BlockSpec(memory_space=pltpu.SMEM)
ANY = pl.BlockSpec(memory_space=pl.ANY)


def column_probe():
    hashed = (7919 * (np.arange(FF, dtype=np.int64) + 1)) % PRIME
    return ((hashed % 511 - 255) / 256.0).astype(np.float32).reshape(GROUPS, COLS)


def turn_kernel(w_ref, t_ref):
    def step(s, _):
        at = pl.multiple_of(s * 128, 128)
        t_ref[pl.ds(at, 128), :] = w_ref[:, pl.ds(at, 128)].T.astype(jnp.float32)
        return 0

    lax.fori_loop(0, FF // 128, step, 0, unroll=4)


def turn(weights):
    return pl.pallas_call(
        turn_kernel,
        out_shape=jax.ShapeDtypeStruct((FF, ROWS), jnp.float32),
        in_specs=[VMEM],
        out_specs=VMEM,
        compiler_params=pltpu.CompilerParams(vmem_limit_bytes=8 * MIB),
        cost_estimate=pl.CostEstimate(flops=0, bytes_accessed=6 * MIB, transcendentals=0),
        name="turn",
    )(weights)


def pieces(value):
    high = value.astype(jnp.bfloat16).astype(jnp.float32)
    rest = value - high
    middle = rest.astype(jnp.bfloat16).astype(jnp.float32)
    return [high, middle, rest - middle]


def pick_kernel(order_ref, t_ref, gains_ref, own_ref, probe_ref, out_ref, held, sem, *, per):
    mean = jnp.sum(gains_ref[...], axis=0, keepdims=True) * (1.0 / 8.0)
    scale = own_ref[...] / mean
    sublane = lax.broadcasted_iota(jnp.int32, (8, 128), 0)
    masks = [sublane == i for i in range(8)]

    def block(d):
        tiles = []
        for j in range(0, COLS, 8):
            tile = t_ref[pl.ds(order_ref[d * COLS + j], 8, stride=0), :]
            for i in range(1, 8):
                row = t_ref[pl.ds(order_ref[d * COLS + j + i], 8, stride=0), :]
                tile = jnp.where(masks[i], row, tile)
            tiles.append(tile)
        return jnp.concatenate(tiles, axis=0)

    def step(p, total):
        picked = [block(p * per + q) for q in range(per)]
        for q in range(per):
            d = p * per + q
            folded = (picked[q] * scale).astype(jnp.bfloat16).T
            held[d, 0:ROWS, :] = folded
            total = total + folded.astype(jnp.float32) * probe_ref[pl.ds(d, 1), :]
        return total

    total = lax.fori_loop(0, GROUPS // per, step, jnp.zeros((ROWS, COLS), jnp.float32))
    printed = jnp.sum(total.T, axis=0, keepdims=True)
    rows = pieces(printed) + pieces(mean) + [jnp.zeros((2, 128), jnp.float32)]
    extra = jnp.concatenate(rows, axis=0).astype(jnp.bfloat16)

    def fill(d, _):
        held[d, ROWS:SENT, :] = extra
        return 0

    lax.fori_loop(0, GROUPS, fill, 0, unroll=8)
    copy = pltpu.make_async_copy(held, out_ref, sem)
    copy.start()
    copy.wait()


def pick(order, turned, gains, own):
    return pl.pallas_call(
        functools.partial(pick_kernel, per=4),
        out_shape=jax.ShapeDtypeStruct((GROUPS, SENT, COLS), jnp.bfloat16),
        in_specs=[SMEM, VMEM, VMEM, VMEM, VMEM],
        out_specs=ANY,
        scratch_shapes=[
            pltpu.VMEM((GROUPS, SENT, COLS), jnp.bfloat16),
            pltpu.SemaphoreType.DMA,
        ],
        compiler_params=pltpu.CompilerParams(vmem_limit_bytes=8 * MIB),
        cost_estimate=pl.CostEstimate(flops=0, bytes_accessed=24 * MIB, transcendentals=0),
        name="pick",
    )(order, turned, gains, own, column_probe())


def reduced(value):
    left = value - (value.astype(jnp.float32) * (1.0 / PRIME)).astype(jnp.int32) * PRIME
    left = jnp.where(left < 0, left + PRIME, left)
    return jnp.where(left >= PRIME, left - PRIME, left)


def probes_kernel(layer_ref, seeds_ref, out_ref):
    lane = lax.broadcasted_iota(jnp.int32, (8, 128), 1)

    def rows(j, _):
        at = pl.multiple_of(j * 16, 16)
        seeds = [jnp.broadcast_to(seeds_ref[pl.ds(at + 8 * u, 8), :], (8, 128)) for u in range(2)]
        steps = [reduced(seed * 128) for seed in seeds]
        for b in range(LAYERS):
            hashed = [reduced(seed * (layer_ref[b] * D + 1 + lane)) for seed in seeds]
            for c in range(0, D, 128):
                made = []
                for u in range(2):
                    value = hashed[u]
                    small = lax.shift_right_logical(value, 9) + (value & 511)
                    small = jnp.where(small >= 511, small - (511 + 255), small - 255)
                    made.append(small.astype(jnp.float32) * (1.0 / 256.0))
                    after = value + steps[u] - PRIME
                    hashed[u] = jnp.where(after < 0, after + PRIME, after)
                out_ref[pl.ds(at, 16), b * D + c : b * D + c + 128] = jnp.concatenate(
                    made, axis=0
                ).astype(jnp.bfloat16)
        return 0

    lax.fori_loop(0, PROBES // 16, rows, 0)


def make_probes(layer_order, seeds):
    return pl.pallas_call(
        probes_kernel,
        out_shape=jax.ShapeDtypeStruct((PROBES, LAYERS * D), jnp.bfloat16),
        in_specs=[SMEM, VMEM],
        out_specs=VMEM,
        compiler_params=pltpu.CompilerParams(vmem_limit_bytes=8 * MIB),
        cost_estimate=pl.CostEstimate(flops=0, bytes_accessed=64 * MIB, transcendentals=0),
        name="probes",
    )(layer_order, seeds.reshape(PROBES, 1))


def sketch_kernel(
    layer_ref, in_ref, probes_ref, out_ref, sums_ref, print_ref, gain_ref, total, turned, sem
):
    per_layer = GROUPS // LAYERS

    def placed(b):
        return pltpu.make_async_copy(
            in_ref.at[pl.ds(per_layer * b, per_layer), pl.ds(0, ROWS), :],
            out_ref.at[pl.ds(layer_ref[b] * per_layer, per_layer)],
            sem,
        )

    for b in range(LAYERS):
        placed(b).start()
    extra = in_ref[:, ROWS:SENT, :].astype(jnp.float32)
    mean = extra[:, 3, :] + extra[:, 4, :] + extra[:, 5, :]
    for b in range(LAYERS):
        at = pl.multiple_of(layer_ref[b] * per_layer, per_layer)
        gain_ref[pl.ds(at, per_layer), :] = mean[per_layer * b : per_layer * (b + 1)]
    row = lax.broadcasted_iota(jnp.int32, extra.shape, 1)
    printed = jnp.where(row < 3, extra, 0.0).reshape(GROUPS * 8, ROWS)
    for j in range(4):
        turned[j] = printed[j * 128 : (j + 1) * 128].T
    lane = lax.broadcasted_iota(jnp.int32, (ROWS, 128), 1) // 8

    for b in range(LAYERS):
        blocks = []
        for g in range(per_layer):
            beside = jnp.where(lane == g, turned[b], 0.0).astype(jnp.bfloat16)
            blocks.append(jnp.concatenate([in_ref[b * per_layer + g, 0:ROWS, :], beside], axis=1))
        product = jnp.dot(
            probes_ref[:, b * D : (b + 1) * D],
            jnp.concatenate(blocks, axis=0),
            preferred_element_type=jnp.float32,
        )
        if b == 0:
            total[...] = product
        else:
            total[...] += product
    sums_ref[...] = total[:, 0:COLS]
    for j in range(PROBES // 128):
        part = total[j * 128 : (j + 1) * 128, COLS:].T
        print_ref[:, j * 128 : (j + 1) * 128] = jnp.sum(part, axis=0, keepdims=True) * FF ** (-0.5)
    for b in range(LAYERS):
        placed(b).wait()


def sketch(layer_order, arrived, probes):
    return pl.pallas_call(
        sketch_kernel,
        out_shape=(
            jax.ShapeDtypeStruct((GROUPS, ROWS, COLS), jnp.bfloat16),
            jax.ShapeDtypeStruct((PROBES, COLS), jnp.float32),
            jax.ShapeDtypeStruct((1, PROBES), jnp.float32),
            jax.ShapeDtypeStruct((GROUPS, ROWS), jnp.float32),
        ),
        in_specs=[SMEM, VMEM, VMEM],
        out_specs=(ANY, VMEM, VMEM, VMEM),
        scratch_shapes=[
            pltpu.VMEM((PROBES, 256), jnp.float32),
            pltpu.VMEM((4, ROWS, 128), jnp.float32),
            pltpu.SemaphoreType.DMA,
        ],
        compiler_params=pltpu.CompilerParams(vmem_limit_bytes=12 * MIB),
        cost_estimate=pl.CostEstimate(
            flops=2 * PROBES * LAYERS * D * COLS, bytes_accessed=22 * MIB, transcendentals=0
        ),
        name="sketch",
    )(layer_order, arrived, probes)


def local(branch_weights, branch_gains, column_order, layer_order, probe_seeds):
    gains = lax.all_to_all(
        jnp.broadcast_to(branch_gains[None], (8, 1, ROWS)), "expert", 0, 0, tiled=True
    ).reshape(8, ROWS)
    turned = turn(branch_weights[0])
    blocks = pick(column_order[0], turned, gains, branch_gains)
    blocks, seeds = lax.optimization_barrier((blocks, probe_seeds))
    arrived = lax.all_to_all(blocks, STACK, 0, 0, tiled=True)
    probes = make_probes(layer_order, seeds)
    ordered, sums, printed, shared = sketch(layer_order, arrived, probes)
    return (
        ordered.reshape(1, LAYERS * D, COLS),
        sums[None],
        printed.reshape(1, PROBES),
        shared.reshape(LAYERS * D),
    )


def solution(mesh):
    return jax.shard_map(
        local,
        mesh=mesh,
        in_specs=(
            P("expert", STACK, None),
            P("expert", STACK),
            P("expert", None),
            P(),
            P(),
        ),
        out_specs=(
            P("expert", None, STACK),
            P("expert", None, STACK),
            P("expert", None),
            P(),
        ),
        check_vma=False,
    )
```

time: 209 us -> 114 us (0.55)
  the two profiles are of different devices: /device:TPU:8 before, /device:TPU:1 now
where the time goes in v1:
time: 114 us
  Pallas kernels  40.5 us (36%)
  waiting for transfers between devices  30.6 us (27%)
  starting transfers between devices  23.1 us (20%)
  local copies, waits for them, and re-layouts  18.7 us (16%)
    all_to_all x1, waiting for transfers between devices, local(): arrived = lax.all_to_all(blocks, STACK, 0, 0, tiled=True)  30.6 us
    pallas_call x1, Pallas kernels, make_probes(): pl.pallas_call(probes_kernel, out_shape=jax.ShapeDtypeStruct((PROBES, LAY...  21.8 us
    all_to_all x1, starting transfers between devices, local(): arrived = lax.all_to_all(blocks, STACK, 0, 0, tiled=True)  17.3 us
    unnamed x20, local copies, waits for them, and re-layouts  17.2 us
    pallas_call x1, Pallas kernels, pick(): pl.pallas_call(functools.partial(pick_kernel, per=4), out_shape=jax.Shape...  10.1 us
    pallas_call x1, Pallas kernels, sketch(): pl.pallas_call(sketch_kernel, out_shape=(jax.ShapeDtypeStruct((GROUPS, RO...  7.11 us
    all_to_all x1, starting transfers between devices, local(): lax.all_to_all(jnp.broadcast_to(branch_gains[None], (8, 1, ROWS)), 'exper...  5.86 us
  transfers between devices with their start and end apart: 2, of which 1 were waited for; matrix products, arithmetic and copies ran while one was open for 0% of the time, Pallas kernels for 20%

profile of v1, /device:TPU:1, one launch (start us, length us, event | category | flops | bytes accessed | tf_op | source)
XLA Modules:
  0.0 113.7 jit_solution(853146782124951351)
XLA Ops:
  0.6 1.3 %broadcast_in_dim.12 = f32[8,1,128]{2,1,0:T(1,128)} broadcast(f32[128]{0:T(128)} %bitcast.11), dimensions={2} | broadcast | bytes 4608 | tf_op jit(solution)/shard_map/broadcast_in_dim | solution.py:234
  1.9 5.9 %all-to-all-start = ((f32[8,1,128]{2,1,0:T(1,128)}), f32[8,1,128]{2,1,0:T(1,128)S(1)}, u32[]{:S(2)}, u32[]{:S(2)}) async-start(f32[8,1,128]{2,1,0:T(1,128)} %broadcast_in_dim.12), calls=%async_computation | async-start | bytes 8192 | tf_op jit(solution)/shard_map/all_to_all | solution.py:233
  7.7 0.0 copy-start.4
  7.7 1.6 %copy-done.4 = bf16[1,128,8192]{2,1,0:T(8,128)(2,1)S(1)} copy-done((bf16[1,128,8192]{2,1,0:T(8,128)(2,1)S(1)}, bf16[1,128,8192]{2,1,0:T(8,128)(2,1)}, u32[]{:S(2)}) %copy-start.4) | copy-done | bytes 2097176
  9.3 0.0 copy-start.5
  9.3 0.0 copy-start.6
  9.3 0.0 copy-start.8
  9.3 1.4 %turn.1.t_ref = f32[8192,128]{1,0:T(8,128)S(1)} custom-call(bf16[128,8192]{1,0:T(8,128)(2,1)S(1)} %bitcast.8), custom_call_target="tpu_custom_call" | custom-call | bytes 6291456 | tf_op jit(solution)/shard_map/turn/pallas_call | solution.py:43
  10.8 0.0 copy-start.2
  10.8 1.9 %copy-done.2 = f32[8192,128]{1,0:T(8,128)} copy-done((f32[8192,128]{1,0:T(8,128)}, f32[8192,128]{1,0:T(8,128)S(1)}, u32[]{:S(2)}) %copy-start.2) | copy-done | bytes 4194328
  12.7 0.0 all-to-all-done
  12.7 0.0 copy-done.5
  12.7 0.0 copy-done.6
  12.7 0.0 copy-done.8
  12.8 0.0 copy-start.3
  12.8 2.2 %copy-done.3 = f32[8192,128]{1,0:T(8,128)S(1)} copy-done((f32[8192,128]{1,0:T(8,128)S(1)}, f32[8192,128]{1,0:T(8,128)}, u32[]{:S(2)}) %copy-start.3) | copy-done | bytes 4194328
  14.9 10.1 %pick.1 = bf16[64,136,128]{2,1,0:T(8,128)(2,1)} custom-call(s32[8192]{0:T(1024)S(1)} %bitcast.9, f32[8192,128]{1,0:T(8,128)S(1)} %copy-done.3, f32[8,128]{1,0:T(8,128)S(1)} %bitcast.10, f32[1,128]{1,0:T(1,128)S(1)} %copy-done.8, f32[64,128]{1,0:T(8,128)S(1)} %copy-done.6), custom_call_target="tpu_custom_call" | custom-call | bytes 25165824 | tf_op jit(solution)/shard_map/pick/pallas_call | solution.py:102
  25.1 0.0 copy-start.9
  25.1 0.0 copy-start.7
  25.1 17.3 %all-to-all-start.1 = ((bf16[64,136,128]{2,1,0:T(8,128)(2,1)}), bf16[64,136,128]{2,1,0:T(8,128)(2,1)S(1)}, u32[]{:S(2)}, u32[]{:S(2)}) async-start(bf16[64,136,128]{2,1,0:T(8,128)(2,1)} %pick.1), calls=%async_computation.1 | async-start | bytes 4456448 | tf_op jit(solution)/shard_map/all_to_all | solution.py:239
  42.4 0.0 copy-done.9
  42.4 0.2 copy.11.seeds_ref
  42.6 0.0 copy-done.7
  42.6 21.8 %probes.1.probes_ref = bf16[1024,8192]{1,0:T(8,128)(2,1)S(1)} custom-call(s32[4]{0:T(128)S(1)} %copy-done.7, s32[1024,1]{1,0:T(8,128)S(1)} %copy.11.seeds_ref), custom_call_target="tpu_custom_call" | custom-call | bytes 67108864 | tf_op jit(solution)/shard_map/probes/pallas_call | solution.py:150
  64.5 0.0 copy-start
  64.5 5.7 %copy-done = bf16[1024,8192]{1,0:T(8,128)(2,1)} copy-done((bf16[1024,8192]{1,0:T(8,128)(2,1)}, bf16[1024,8192]{1,0:T(8,128)(2,1)S(1)}, u32[]{:S(2)}) %copy-start) | copy-done | bytes 16777240
  70.2 30.6 %all-to-all-done.1.in_ref = bf16[64,136,128]{2,1,0:T(8,128)(2,1)S(1)} async-done(((bf16[64,136,128]{2,1,0:T(8,128)(2,1)}), bf16[64,136,128]{2,1,0:T(8,128)(2,1)S(1)}, u32[]{:S(2)}, u32[]{:S(2)}) %all-to-all-start.1) | async-done | bytes 2228256 | tf_op jit(solution)/shard_map/all_to_all | solution.py:239
  100.8 0.0 copy-start.1
  100.8 5.8 %copy-done.1 = bf16[1024,8192]{1,0:T(8,128)(2,1)S(1)} copy-done((bf16[1024,8192]{1,0:T(8,128)(2,1)S(1)}, bf16[1024,8192]{1,0:T(8,128)(2,1)}, u32[]{:S(2)}) %copy-start.1) | copy-done | bytes 16777240
  106.6 7.1 %sketch.1 = (bf16[64,128,128]{2,1,0:T(8,128)(2,1)}, f32[1024,128]{1,0:T(8,128)}, f32[1,1024]{1,0:T(1,128)}, f32[64,128]{1,0:T(8,128)}) custom-call(s32[4]{0:T(128)S(1)} %copy-done.7, bf16[64,136,128]{2,1,0:T(8,128)(2,1)S(1)} %all-to-all-done.1.in_ref, bf16[1024,8192]{1,0:T(8,128)(2,1)S(1)} %copy-done.1), custom_call_target="tpu_custom_call" | custom-call | flops 2147483648 | bytes 23068672 | tf_op jit(solution)/shard_map/sketch/pallas_call | solution.py:209
Async XLA Ops:
  1.9 10.9 %all-to-all-start = ((f32[8,1,128]{2,1,0:T(1,128)}), f32[8,1,128]{2,1,0:T(1,128)S(1)}, u32[]{:S(2)}, u32[]{:S(2)}) async-start(f32[8,1,128]{2,1,0:T(1,128)} %broadcast_in_dim.12), calls=%async_computation | async-start | bytes 8192 | tf_op jit(solution)/shard_map/all_to_all | solution.py:233
  7.7 1.6 %copy-start.4 = (bf16[1,128,8192]{2,1,0:T(8,128)(2,1)S(1)}, bf16[1,128,8192]{2,1,0:T(8,128)(2,1)}, u32[]{:S(2)}) copy-start(bf16[1,128,8192]{2,1,0:T(8,128)(2,1)} %param.6) | copy-start | bytes 6291460
  9.3 3.4 %copy-start.5 = (s32[1,8192]{1,0:T(1,128)S(1)}, s32[1,8192]{1,0:T(1,128)}, u32[]{:S(2)}) copy-start(s32[1,8192]{1,0:T(1,128)} %param.8) | copy-start | bytes 98308
  9.3 3.4 %copy-start.6 = (f32[64,128]{1,0:T(8,128)S(1)}, f32[64,128]{1,0:T(8,128)}, u32[]{:S(2)}) copy-start(f32[64,128]{1,0:T(8,128)} %constant.2.clone.probe_ref) | copy-start | bytes 98308
  9.3 3.4 %copy-start.8 = (f32[1,128]{1,0:T(1,128)S(1)}, f32[1,128]{1,0:T(1,128)}, u32[]{:S(2)}) copy-start(f32[1,128]{1,0:T(1,128)} %own_ref.1) | copy-start | bytes 1540
  10.8 1.9 %copy-start.2 = (f32[8192,128]{1,0:T(8,128)}, f32[8192,128]{1,0:T(8,128)S(1)}, u32[]{:S(2)}) copy-start(f32[8192,128]{1,0:T(8,128)S(1)} %turn.1.t_ref) | copy-start | bytes 12582916
  12.8 2.2 %copy-start.3 = (f32[8192,128]{1,0:T(8,128)S(1)}, f32[8192,128]{1,0:T(8,128)}, u32[]{:S(2)}) copy-start(f32[8192,128]{1,0:T(8,128)} %copy-done.2) | copy-start | bytes 12582916
  25.1 17.3 %copy-start.9 = (s32[1024]{0:T(1024)S(1)}, s32[1024]{0:T(1024)}, u32[]{:S(2)}) copy-start(s32[1024]{0:T(1024)} %param.10) | copy-start | bytes 12292
  25.1 17.5 %copy-start.7 = (s32[4]{0:T(128)S(1)}, s32[4]{0:T(128)}, u32[]{:S(2)}) copy-start(s32[4]{0:T(128)} %layer_ref.3) | copy-start | bytes 52
  25.1 75.8 %all-to-all-start.1 = ((bf16[64,136,128]{2,1,0:T(8,128)(2,1)}), bf16[64,136,128]{2,1,0:T(8,128)(2,1)S(1)}, u32[]{:S(2)}, u32[]{:S(2)}) async-start(bf16[64,136,128]{2,1,0:T(8,128)(2,1)} %pick.1), calls=%async_computation.1 | async-start | bytes 4456448 | tf_op jit(solution)/shard_map/all_to_all | solution.py:239
  64.5 5.7 %copy-start = (bf16[1024,8192]{1,0:T(8,128)(2,1)}, bf16[1024,8192]{1,0:T(8,128)(2,1)S(1)}, u32[]{:S(2)}) copy-start(bf16[1024,8192]{1,0:T(8,128)(2,1)S(1)} %probes.1.probes_ref) | copy-start | bytes 50331652
  100.8 5.8 %copy-start.1 = (bf16[1024,8192]{1,0:T(8,128)(2,1)S(1)}, bf16[1024,8192]{1,0:T(8,128)(2,1)}, u32[]{:S(2)}) copy-start(bf16[1024,8192]{1,0:T(8,128)(2,1)} %copy-done) | copy-start | bytes 50331652

commit v2 on v1

--- a/solution.py
+++ b/solution.py
@@ -30,25 +30,85 @@
     return ((hashed % 511 - 255) / 256.0).astype(np.float32).reshape(GROUPS, COLS)
 
 
-def turn_kernel(w_ref, t_ref):
+def gather_kernel(
+    order_ref, w_ref, out_ref, packed, pairs, rows, turned, held, sem, in_sem, out_sem
+):
+    parts = 4
+    wide = FF // parts
+
+    def fetch(c):
+        at = pl.ds(c * wide, wide)
+        return pltpu.make_async_copy(w_ref.at[:, at], rows.at[:, at], in_sem.at[c])
+
+    for c in range(parts):
+        fetch(c).start()
+    half = GROUPS // 2
+    packed[...] = order_ref[0:half, :] + order_ref[half:, :] * 65536
+    copy = pltpu.make_async_copy(packed, pairs, sem)
+    copy.start()
+    for c in range(parts):
+        fetch(c).wait()
+
+        def turn(s, _):
+            at = pl.multiple_of(c * wide + s * 128, 128)
+            turned[pl.ds(at, 128), :] = rows[:, pl.ds(at, 128)].T.astype(jnp.float32)
+            return 0
+
+        lax.fori_loop(0, wide // 128, turn, 0, unroll=4)
+    copy.wait()
+    sublane = lax.broadcasted_iota(jnp.int32, (8, 128), 0)
+    masks = [sublane == i for i in range(8)]
+
+    def send(at, count):
+        return pltpu.make_async_copy(
+            held.at[pl.ds(at, count)], out_ref.at[pl.ds(at, count)], out_sem
+        )
+
+    def both(p):
+        tiles = ([], [])
+        for j in range(0, COLS, 8):
+            made = [None, None]
+            for i in range(8):
+                word = pairs[p, j + i]
+                for u, column in enumerate((word & 65535, lax.shift_right_logical(word, 16))):
+                    row = turned[pl.ds(column, 8, stride=0), :]
+                    made[u] = row if i == 0 else jnp.where(masks[i], row, made[u])
+            for u in range(2):
+                tiles[u].append(made[u])
+        for u in range(2):
+            held[p + half * u] = jnp.concatenate(tiles[u], axis=0).astype(jnp.bfloat16).T
+
     def step(s, _):
-        at = pl.multiple_of(s * 128, 128)
-        t_ref[pl.ds(at, 128), :] = w_ref[:, pl.ds(at, 128)].T.astype(jnp.float32)
+        for q in range(4):
+            both(s * 4 + q)
+        send(s * 4, 4).start()
+        send(s * 4 + half, 4).start()
         return 0
 
-    lax.fori_loop(0, FF // 128, step, 0, unroll=4)
-
-
-def turn(weights):
+    lax.fori_loop(0, half // 4, step, 0)
+    send(0, GROUPS).wait()
+
+
+def gather(order, weights):
     return pl.pallas_call(
-        turn_kernel,
-        out_shape=jax.ShapeDtypeStruct((FF, ROWS), jnp.float32),
-        in_specs=[VMEM],
-        out_specs=VMEM,
-        compiler_params=pltpu.CompilerParams(vmem_limit_bytes=8 * MIB),
-        cost_estimate=pl.CostEstimate(flops=0, bytes_accessed=6 * MIB, transcendentals=0),
-        name="turn",
-    )(weights)
+        gather_kernel,
+        out_shape=jax.ShapeDtypeStruct((GROUPS, ROWS, COLS), jnp.bfloat16),
+        in_specs=[VMEM, ANY],
+        out_specs=ANY,
+        scratch_shapes=[
+            pltpu.VMEM((GROUPS // 2, COLS), jnp.int32),
+            pltpu.SMEM((GROUPS // 2, COLS), jnp.int32),
+            pltpu.VMEM((ROWS, FF), jnp.bfloat16),
+            pltpu.VMEM((FF, ROWS), jnp.float32),
+            pltpu.VMEM((GROUPS, ROWS, COLS), jnp.bfloat16),
+            pltpu.SemaphoreType.DMA,
+            pltpu.SemaphoreType.DMA((4,)),
+            pltpu.SemaphoreType.DMA,
+        ],
+        compiler_params=pltpu.CompilerParams(vmem_limit_bytes=59 * MIB),
+        cost_estimate=pl.CostEstimate(flops=0, bytes_accessed=24 * MIB, transcendentals=0),
+        name="gather",
+    )(order.reshape(GROUPS, COLS), weights)
 
 
 def pieces(value):
@@ -58,60 +118,61 @@
     return [high, middle, rest - middle]
 
 
-def pick_kernel(order_ref, t_ref, gains_ref, own_ref, probe_ref, out_ref, held, sem, *, per):
+def fold_kernel(raw_ref, gains_ref, own_ref, probe_ref, out_ref, rows, held, extra, in_sem, sem):
+    parts, count = 4, GROUPS // 4
+
+    def fetch(c):
+        at = pl.ds(c * count, count)
+        return pltpu.make_async_copy(raw_ref.at[at], rows.at[at], in_sem.at[c])
+
+    def send(c):
+        at = pl.ds(c * count, count)
+        return pltpu.make_async_copy(held.at[at], out_ref.at[at, pl.ds(0, ROWS), :], sem.at[c])
+
+    for c in range(parts):
+        fetch(c).start()
     mean = jnp.sum(gains_ref[...], axis=0, keepdims=True) * (1.0 / 8.0)
-    scale = own_ref[...] / mean
-    sublane = lax.broadcasted_iota(jnp.int32, (8, 128), 0)
-    masks = [sublane == i for i in range(8)]
-
-    def block(d):
-        tiles = []
-        for j in range(0, COLS, 8):
-            tile = t_ref[pl.ds(order_ref[d * COLS + j], 8, stride=0), :]
-            for i in range(1, 8):
-                row = t_ref[pl.ds(order_ref[d * COLS + j + i], 8, stride=0), :]
-                tile = jnp.where(masks[i], row, tile)
-            tiles.append(tile)
-        return jnp.concatenate(tiles, axis=0)
-
-    def step(p, total):
-        picked = [block(p * per + q) for q in range(per)]
-        for q in range(per):
-            d = p * per + q
-            folded = (picked[q] * scale).astype(jnp.bfloat16).T
-            held[d, 0:ROWS, :] = folded
-            total = total + folded.astype(jnp.float32) * probe_ref[pl.ds(d, 1), :]
-        return total
-
-    total = lax.fori_loop(0, GROUPS // per, step, jnp.zeros((ROWS, COLS), jnp.float32))
+    scale = jnp.broadcast_to(own_ref[...] / mean, (COLS, ROWS)).T
+    total = jnp.zeros((ROWS, COLS), jnp.float32)
+    for c in range(parts):
+        fetch(c).wait()
+
+        def step(s, total):
+            d = c * count + s
+            folded = (rows[d].astype(jnp.float32) * scale).astype(jnp.bfloat16)
+            held[d] = folded
+            return total + folded.astype(jnp.float32) * probe_ref[pl.ds(d, 1), :]
+
+        total = lax.fori_loop(0, count, step, total, unroll=4)
+        send(c).start()
     printed = jnp.sum(total.T, axis=0, keepdims=True)
-    rows = pieces(printed) + pieces(mean) + [jnp.zeros((2, 128), jnp.float32)]
-    extra = jnp.concatenate(rows, axis=0).astype(jnp.bfloat16)
-
-    def fill(d, _):
-        held[d, ROWS:SENT, :] = extra
-        return 0
-
-    lax.fori_loop(0, GROUPS, fill, 0, unroll=8)
-    copy = pltpu.make_async_copy(held, out_ref, sem)
+    added = pieces(printed) + pieces(mean) + [jnp.zeros((2, ROWS), jnp.float32)]
+    added = jnp.concatenate(added, axis=0).astype(jnp.bfloat16)
+    extra[...] = jnp.broadcast_to(added[None], extra.shape)
+    copy = pltpu.make_async_copy(extra, out_ref.at[:, pl.ds(ROWS, SENT - ROWS), :], sem.at[parts])
     copy.start()
+    for c in range(parts):
+        send(c).wait()
     copy.wait()
 
 
-def pick(order, turned, gains, own):
+def fold(raw, gains, own):
     return pl.pallas_call(
-        functools.partial(pick_kernel, per=4),
+        fold_kernel,
         out_shape=jax.ShapeDtypeStruct((GROUPS, SENT, COLS), jnp.bfloat16),
-        in_specs=[SMEM, VMEM, VMEM, VMEM, VMEM],
+        in_specs=[ANY, VMEM, VMEM, VMEM],
         out_specs=ANY,
         scratch_shapes=[
-            pltpu.VMEM((GROUPS, SENT, COLS), jnp.bfloat16),
-            pltpu.SemaphoreType.DMA,
+            pltpu.VMEM((GROUPS, ROWS, COLS), jnp.bfloat16),
+            pltpu.VMEM((GROUPS, ROWS, COLS), jnp.bfloat16),
+            pltpu.VMEM((GROUPS, SENT - ROWS, COLS), jnp.bfloat16),
+            pltpu.SemaphoreType.DMA((4,)),
+            pltpu.SemaphoreType.DMA((5,)),
         ],
-        compiler_params=pltpu.CompilerParams(vmem_limit_bytes=8 * MIB),
-        cost_estimate=pl.CostEstimate(flops=0, bytes_accessed=24 * MIB, transcendentals=0),
-        name="pick",
-    )(order, turned, gains, own, column_probe())
+        compiler_params=pltpu.CompilerParams(vmem_limit_bytes=59 * MIB),
+        cost_estimate=pl.CostEstimate(flops=0, bytes_accessed=5 * MIB, transcendentals=0),
+        name="fold",
+    )(raw, gains, own, column_probe())
 
 
 def reduced(value):
@@ -143,16 +204,21 @@
                 ).astype(jnp.bfloat16)
         return 0
 
-    lax.fori_loop(0, PROBES // 16, rows, 0)
+    lax.fori_loop(0, out_ref.shape[0] // 16, rows, 0)
 
 
 def make_probes(layer_order, seeds):
+    rows = PROBES // 8
     return pl.pallas_call(
         probes_kernel,
         out_shape=jax.ShapeDtypeStruct((PROBES, LAYERS * D), jnp.bfloat16),
-        in_specs=[SMEM, VMEM],
-        out_specs=VMEM,
-        compiler_params=pltpu.CompilerParams(vmem_limit_bytes=8 * MIB),
+        grid_spec=pltpu.PrefetchScalarGridSpec(
+            num_scalar_prefetch=1,
+            grid=(8,),
+            in_specs=[pl.BlockSpec((rows, 1), lambda j, order: (j, 0))],
+            out_specs=pl.BlockSpec((rows, LAYERS * D), lambda j, order: (j, 0)),
+        ),
+        compiler_params=pltpu.CompilerParams(vmem_limit_bytes=56 * MIB),
         cost_estimate=pl.CostEstimate(flops=0, bytes_accessed=64 * MIB, transcendentals=0),
         name="probes",
     )(layer_order, seeds.reshape(PROBES, 1))
@@ -233,8 +299,8 @@
     gains = lax.all_to_all(
         jnp.broadcast_to(branch_gains[None], (8, 1, ROWS)), "expert", 0, 0, tiled=True
     ).reshape(8, ROWS)
-    turned = turn(branch_weights[0])
-    blocks = pick(column_order[0], turned, gains, branch_gains)
+    raw = gather(column_order[0], branch_weights[0])
+    blocks = fold(raw, gains, branch_gains)
     blocks, seeds = lax.optimization_barrier((blocks, probe_seeds))
     arrived = lax.all_to_all(blocks, STACK, 0, 0, tiled=True)
     probes = make_probes(layer_order, seeds)

time: 114 us -> 111 us (0.974)
  the two profiles are of different devices: /device:TPU:1 before, /device:TPU:17 now
where the time goes in v2:
time: 111 us
  Pallas kernels  46 us (41%)
  waiting for transfers between devices  34.1 us (31%)
  starting transfers between devices  21.2 us (19%)
  local copies, waits for them, and re-layouts  8.65 us (8%)
    all_to_all x1, waiting for transfers between devices, local(): arrived = lax.all_to_all(blocks, STACK, 0, 0, tiled=True)  34.1 us
    pallas_call x1, Pallas kernels, make_probes(): pl.pallas_call(probes_kernel, out_shape=jax.ShapeDtypeStruct((PROBES, LAY...  24.4 us
    all_to_all x1, starting transfers between devices, local(): arrived = lax.all_to_all(blocks, STACK, 0, 0, tiled=True)  16.2 us
    pallas_call x1, Pallas kernels, gather(): pl.pallas_call(gather_kernel, out_shape=jax.ShapeDtypeStruct((GROUPS, ROW...  10.9 us
    pallas_call x1, Pallas kernels, sketch(): pl.pallas_call(sketch_kernel, out_shape=(jax.ShapeDtypeStruct((GROUPS, RO...  7.1 us
    unnamed x8, local copies, waits for them, and re-layouts  6.37 us
    all_to_all x1, starting transfers between devices, local(): lax.all_to_all(jnp.broadcast_to(branch_gains[None], (8, 1, ROWS)), 'exper...  5.03 us
    pallas_call x1, Pallas kernels, fold(): pl.pallas_call(fold_kernel, out_shape=jax.ShapeDtypeStruct((GROUPS, SENT,...  3.61 us
  transfers between devices with their start and end apart: 2, of which 1 were waited for; matrix products, arithmetic and copies ran while one was open for 1% of the time, Pallas kernels for 32%

profile of v2, /device:TPU:17, one launch (start us, length us, event | category | flops | bytes accessed | tf_op | source)
XLA Modules:
  0.0 110.7 jit_solution(15745047627726473235)
XLA Ops:
  0.6 1.3 %broadcast_in_dim.12 = f32[8,1,128]{2,1,0:T(1,128)} broadcast(f32[128]{0:T(128)} %bitcast.12), dimensions={2} | broadcast | bytes 4608 | tf_op jit(solution)/shard_map/broadcast_in_dim | solution.py:300
  1.9 5.0 %all-to-all-start = ((f32[8,1,128]{2,1,0:T(1,128)}), f32[8,1,128]{2,1,0:T(1,128)S(1)}, u32[]{:S(2)}, u32[]{:S(2)}) async-start(f32[8,1,128]{2,1,0:T(1,128)} %broadcast_in_dim.12), calls=%async_computation | async-start | bytes 8192 | tf_op jit(solution)/shard_map/all_to_all | solution.py:299
  6.9 10.9 %gather.1.raw_ref = bf16[64,128,128]{2,1,0:T(8,128)(2,1)} custom-call(s32[64,128]{1,0:T(8,128)} %bitcast.9, bf16[128,8192]{1,0:T(8,128)(2,1)} %bitcast.8), custom_call_target="tpu_custom_call" | custom-call | bytes 25165824 | tf_op jit(solution)/shard_map/gather/pallas_call | solution.py:93
  17.8 0.0 all-to-all-done
  17.9 0.0 copy-start.2
  17.9 0.6 copy-done.2
  18.5 3.6 %fold.1 = bf16[64,136,128]{2,1,0:T(8,128)(2,1)} custom-call(bf16[64,128,128]{2,1,0:T(8,128)(2,1)} %gather.1.raw_ref, f32[8,128]{1,0:T(8,128)} %bitcast.10, f32[1,128]{1,0:T(1,128)} %own_ref.1, f32[64,128]{1,0:T(8,128)} %constant.2.clone.probe_ref), custom_call_target="tpu_custom_call" | custom-call | bytes 5242880 | tf_op jit(solution)/shard_map/fold/pallas_call | solution.py:160
  22.1 0.0 copy-start.3
  22.1 16.2 %all-to-all-start.1 = ((bf16[64,136,128]{2,1,0:T(8,128)(2,1)}), bf16[64,136,128]{2,1,0:T(8,128)(2,1)S(1)}, u32[]{:S(2)}, u32[]{:S(2)}) async-start(bf16[64,136,128]{2,1,0:T(8,128)(2,1)} %fold.1), calls=%async_computation.1 | async-start | bytes 4456448 | tf_op jit(solution)/shard_map/all_to_all | solution.py:305
  38.3 0.0 copy-done.3
  38.3 1.0 copy.11.seeds_ref
  39.3 0.0 copy-start.1
  39.3 24.4 %probes.1.probes_ref = bf16[1024,8192]{1,0:T(8,128)(2,1)} custom-call(s32[4]{0:T(128)} %layer_ref.3, s32[1024,1]{1,0:T(8,128)} %copy.11.seeds_ref), custom_call_target="tpu_custom_call" | custom-call | bytes 67108864 | tf_op jit(solution)/shard_map/probes/pallas_call | solution.py:212
  63.7 34.1 %all-to-all-done.1.in_ref = bf16[64,136,128]{2,1,0:T(8,128)(2,1)S(1)} async-done(((bf16[64,136,128]{2,1,0:T(8,128)(2,1)}), bf16[64,136,128]{2,1,0:T(8,128)(2,1)S(1)}, u32[]{:S(2)}, u32[]{:S(2)}) %all-to-all-start.1) | async-done | bytes 2228256 | tf_op jit(solution)/shard_map/all_to_all | solution.py:305
  97.8 0.0 copy-done.1
  97.8 0.0 copy-start
  97.8 5.8 %copy-done = bf16[1024,8192]{1,0:T(8,128)(2,1)S(1)} copy-done((bf16[1024,8192]{1,0:T(8,128)(2,1)S(1)}, bf16[1024,8192]{1,0:T(8,128)(2,1)}, u32[]{:S(2)}) %copy-start) | copy-done | bytes 16777240
  103.6 7.1 %sketch.1 = (bf16[64,128,128]{2,1,0:T(8,128)(2,1)}, f32[1024,128]{1,0:T(8,128)}, f32[1,1024]{1,0:T(1,128)}, f32[64,128]{1,0:T(8,128)}) custom-call(s32[4]{0:T(128)S(1)} %copy-done.1, bf16[64,136,128]{2,1,0:T(8,128)(2,1)S(1)} %all-to-all-done.1.in_ref, bf16[1024,8192]{1,0:T(8,128)(2,1)S(1)} %copy-done), custom_call_target="tpu_custom_call" | custom-call | flops 2147483648 | bytes 23068672 | tf_op jit(solution)/shard_map/sketch/pallas_call | solution.py:275
Async XLA Ops:
  1.9 16.0 %all-to-all-start = ((f32[8,1,128]{2,1,0:T(1,128)}), f32[8,1,128]{2,1,0:T(1,128)S(1)}, u32[]{:S(2)}, u32[]{:S(2)}) async-start(f32[8,1,128]{2,1,0:T(1,128)} %broadcast_in_dim.12), calls=%async_computation | async-start | bytes 8192 | tf_op jit(solution)/shard_map/all_to_all | solution.py:299
  17.9 0.6 copy-start.2
  22.1 16.2 %copy-start.3 = (s32[1024]{0:T(1024)S(1)}, s32[1024]{0:T(1024)}, u32[]{:S(2)}) copy-start(s32[1024]{0:T(1024)} %param.10) | copy-start | bytes 12292
  22.1 75.7 %all-to-all-start.1 = ((bf16[64,136,128]{2,1,0:T(8,128)(2,1)}), bf16[64,136,128]{2,1,0:T(8,128)(2,1)S(1)}, u32[]{:S(2)}, u32[]{:S(2)}) async-start(bf16[64,136,128]{2,1,0:T(8,128)(2,1)} %fold.1), calls=%async_computation.1 | async-start | bytes 4456448 | tf_op jit(solution)/shard_map/all_to_all | solution.py:305
  39.3 58.5 %copy-start.1 = (s32[4]{0:T(128)S(1)}, s32[4]{0:T(128)}, u32[]{:S(2)}) copy-start(s32[4]{0:T(128)} %layer_ref.3) | copy-start | bytes 52
  97.8 5.8 %copy-start = (bf16[1024,8192]{1,0:T(8,128)(2,1)S(1)}, bf16[1024,8192]{1,0:T(8,128)(2,1)}, u32[]{:S(2)}) copy-start(bf16[1024,8192]{1,0:T(8,128)(2,1)} %probes.1.probes_ref) | copy-start | bytes 50331652

commit v3 on v2

--- a/solution.py
+++ b/solution.py
@@ -30,31 +30,22 @@
     return ((hashed % 511 - 255) / 256.0).astype(np.float32).reshape(GROUPS, COLS)
 
 
-def gather_kernel(
-    order_ref, w_ref, out_ref, packed, pairs, rows, turned, held, sem, in_sem, out_sem
-):
-    parts = 4
-    wide = FF // parts
-
-    def fetch(c):
-        at = pl.ds(c * wide, wide)
-        return pltpu.make_async_copy(w_ref.at[:, at], rows.at[:, at], in_sem.at[c])
-
-    for c in range(parts):
-        fetch(c).start()
+def gather_kernel(order_ref, w_ref, out_ref, order, packed, pairs, turned, held, sem, out_sem):
     half = GROUPS // 2
-    packed[...] = order_ref[0:half, :] + order_ref[half:, :] * 65536
-    copy = pltpu.make_async_copy(packed, pairs, sem)
+    fetch = pltpu.make_async_copy(order_ref, order, sem.at[0])
+    fetch.start()
+
+    def turn(s, _):
+        at = pl.multiple_of(s * 128, 128)
+        turned[pl.ds(at, 128), :] = w_ref[:, pl.ds(at, 128)].T.astype(jnp.float32)
+        return 0
+
+    lax.fori_loop(0, FF // 256, turn, 0, unroll=16)
+    fetch.wait()
+    packed[...] = order[0:half, :] + order[half:, :] * 65536
+    copy = pltpu.make_async_copy(packed, pairs, sem.at[1])
     copy.start()
-    for c in range(parts):
-        fetch(c).wait()
-
-        def turn(s, _):
-            at = pl.multiple_of(c * wide + s * 128, 128)
-            turned[pl.ds(at, 128), :] = rows[:, pl.ds(at, 128)].T.astype(jnp.float32)
-            return 0
-
-        lax.fori_loop(0, wide // 128, turn, 0, unroll=4)
+    lax.fori_loop(FF // 256, FF // 128, turn, 0, unroll=16)
     copy.wait()
     sublane = lax.broadcasted_iota(jnp.int32, (8, 128), 0)
     masks = [sublane == i for i in range(8)]
@@ -79,13 +70,13 @@
             held[p + half * u] = jnp.concatenate(tiles[u], axis=0).astype(jnp.bfloat16).T
 
     def step(s, _):
-        for q in range(4):
-            both(s * 4 + q)
-        send(s * 4, 4).start()
-        send(s * 4 + half, 4).start()
+        for q in range(8):
+            both(s * 8 + q)
+        send(s * 8, 8).start()
+        send(s * 8 + half, 8).start()
         return 0
 
-    lax.fori_loop(0, half // 4, step, 0)
+    lax.fori_loop(0, half // 8, step, 0)
     send(0, GROUPS).wait()
 
 
@@ -93,19 +84,18 @@
     return pl.pallas_call(
         gather_kernel,
         out_shape=jax.ShapeDtypeStruct((GROUPS, ROWS, COLS), jnp.bfloat16),
-        in_specs=[VMEM, ANY],
+        in_specs=[ANY, VMEM],
         out_specs=ANY,
         scratch_shapes=[
+            pltpu.VMEM((GROUPS, COLS), jnp.int32),
             pltpu.VMEM((GROUPS // 2, COLS), jnp.int32),
             pltpu.SMEM((GROUPS // 2, COLS), jnp.int32),
-            pltpu.VMEM((ROWS, FF), jnp.bfloat16),
             pltpu.VMEM((FF, ROWS), jnp.float32),
             pltpu.VMEM((GROUPS, ROWS, COLS), jnp.bfloat16),
-            pltpu.SemaphoreType.DMA,
-            pltpu.SemaphoreType.DMA((4,)),
+            pltpu.SemaphoreType.DMA((2,)),
             pltpu.SemaphoreType.DMA,
         ],
-        compiler_params=pltpu.CompilerParams(vmem_limit_bytes=59 * MIB),
+        compiler_params=pltpu.CompilerParams(vmem_limit_bytes=12 * MIB),
         cost_estimate=pl.CostEstimate(flops=0, bytes_accessed=24 * MIB, transcendentals=0),
         name="gather",
     )(order.reshape(GROUPS, COLS), weights)
@@ -118,37 +108,33 @@
     return [high, middle, rest - middle]
 
 
-def fold_kernel(raw_ref, gains_ref, own_ref, probe_ref, out_ref, rows, held, extra, in_sem, sem):
-    parts, count = 4, GROUPS // 4
-
-    def fetch(c):
-        at = pl.ds(c * count, count)
-        return pltpu.make_async_copy(raw_ref.at[at], rows.at[at], in_sem.at[c])
-
-    def send(c):
-        at = pl.ds(c * count, count)
-        return pltpu.make_async_copy(held.at[at], out_ref.at[at, pl.ds(0, ROWS), :], sem.at[c])
-
-    for c in range(parts):
-        fetch(c).start()
+def fold_kernel(raw_ref, gains_ref, own_ref, probe_ref, out_ref, held, extra, sem):
     mean = jnp.sum(gains_ref[...], axis=0, keepdims=True) * (1.0 / 8.0)
     scale = jnp.broadcast_to(own_ref[...] / mean, (COLS, ROWS)).T
+    parts, count = 4, GROUPS // 4
+
+    def send(c):
+        return pltpu.make_async_copy(
+            held.at[pl.ds(c * count, count)],
+            out_ref.at[pl.ds(c * count, count), pl.ds(0, ROWS), :],
+            sem.at[c],
+        )
+
     total = jnp.zeros((ROWS, COLS), jnp.float32)
     for c in range(parts):
-        fetch(c).wait()
 
         def step(s, total):
             d = c * count + s
-            folded = (rows[d].astype(jnp.float32) * scale).astype(jnp.bfloat16)
+            folded = (raw_ref[d].astype(jnp.float32) * scale).astype(jnp.bfloat16)
             held[d] = folded
             return total + folded.astype(jnp.float32) * probe_ref[pl.ds(d, 1), :]
 
         total = lax.fori_loop(0, count, step, total, unroll=4)
         send(c).start()
     printed = jnp.sum(total.T, axis=0, keepdims=True)
-    added = pieces(printed) + pieces(mean) + [jnp.zeros((2, ROWS), jnp.float32)]
-    added = jnp.concatenate(added, axis=0).astype(jnp.bfloat16)
-    extra[...] = jnp.broadcast_to(added[None], extra.shape)
+    rows = pieces(printed) + pieces(mean) + [jnp.zeros((2, ROWS), jnp.float32)]
+    rows = jnp.concatenate(rows, axis=0).astype(jnp.bfloat16)
+    extra[...] = jnp.broadcast_to(rows[None], extra.shape)
     copy = pltpu.make_async_copy(extra, out_ref.at[:, pl.ds(ROWS, SENT - ROWS), :], sem.at[parts])
     copy.start()
     for c in range(parts):
@@ -160,16 +146,14 @@
     return pl.pallas_call(
         fold_kernel,
         out_shape=jax.ShapeDtypeStruct((GROUPS, SENT, COLS), jnp.bfloat16),
-        in_specs=[ANY, VMEM, VMEM, VMEM],
+        in_specs=[VMEM, VMEM, VMEM, VMEM],
         out_specs=ANY,
         scratch_shapes=[
             pltpu.VMEM((GROUPS, ROWS, COLS), jnp.bfloat16),
-            pltpu.VMEM((GROUPS, ROWS, COLS), jnp.bfloat16),
             pltpu.VMEM((GROUPS, SENT - ROWS, COLS), jnp.bfloat16),
-            pltpu.SemaphoreType.DMA((4,)),
             pltpu.SemaphoreType.DMA((5,)),
         ],
-        compiler_params=pltpu.CompilerParams(vmem_limit_bytes=59 * MIB),
+        compiler_params=pltpu.CompilerParams(vmem_limit_bytes=8 * MIB),
         cost_estimate=pl.CostEstimate(flops=0, bytes_accessed=5 * MIB, transcendentals=0),
         name="fold",
     )(raw, gains, own, column_probe())

time: 111 us -> 108 us (0.973)
  Pallas kernels: 46 us -> 41.4 us
  local copies, waits for them, and re-layouts: 8.65 us -> 10.5 us
    pallas_call x1, Pallas kernels: 10.9 us -> 8.09 us  [gather(): pl.pallas_call(gather_kernel, out_shape=jax.ShapeDtypeStruct((GROUPS, ROW...]
    unnamed x8 -> x14, local copies, waits for them, and re-layouts: 6.37 us -> 8.13 us
    pallas_call x1, Pallas kernels: 3.61 us -> 1.85 us  [fold(): pl.pallas_call(fold_kernel, out_shape=jax.ShapeDtypeStruct((GROUPS, SENT,...]
  transfers between devices with their start and end apart: 2 -> 2, of which waited for: 1 -> 1; matrix products, arithmetic and copies ran while one was open for 1% -> 1% of each run, Pallas kernels for 32% -> 30%
where the time goes in v3:
time: 108 us
  Pallas kernels  41.4 us (38%)
  waiting for transfers between devices  34.1 us (32%)
  starting transfers between devices  21.2 us (20%)
  local copies, waits for them, and re-layouts  10.5 us (10%)
    all_to_all x1, waiting for transfers between devices, local(): arrived = lax.all_to_all(blocks, STACK, 0, 0, tiled=True)  34.1 us
    pallas_call x1, Pallas kernels, make_probes(): pl.pallas_call(probes_kernel, out_shape=jax.ShapeDtypeStruct((PROBES, LAY...  24.4 us
    all_to_all x1, starting transfers between devices, local(): arrived = lax.all_to_all(blocks, STACK, 0, 0, tiled=True)  16.2 us
    unnamed x14, local copies, waits for them, and re-layouts  8.13 us
    pallas_call x1, Pallas kernels, gather(): pl.pallas_call(gather_kernel, out_shape=jax.ShapeDtypeStruct((GROUPS, ROW...  8.09 us
    pallas_call x1, Pallas kernels, sketch(): pl.pallas_call(sketch_kernel, out_shape=(jax.ShapeDtypeStruct((GROUPS, RO...  7.11 us
    all_to_all x1, starting transfers between devices, local(): lax.all_to_all(jnp.broadcast_to(branch_gains[None], (8, 1, ROWS)), 'exper...  5.03 us
  transfers between devices with their start and end apart: 2, of which 1 were waited for; matrix products, arithmetic and copies ran while one was open for 1% of the time, Pallas kernels for 30%

profile of v3, /device:TPU:17, one launch (start us, length us, event | category | flops | bytes accessed | tf_op | source)
XLA Modules:
  0.0 108.0 jit_solution(4209383452676484285)
XLA Ops:
  0.6 0.0 copy-start.5
  0.6 1.3 %broadcast_in_dim.12 = f32[8,1,128]{2,1,0:T(1,128)} broadcast(f32[128]{0:T(128)} %bitcast.11), dimensions={2} | broadcast | bytes 4608 | tf_op jit(solution)/shard_map/broadcast_in_dim | solution.py:284
  2.0 5.0 %all-to-all-start = ((f32[8,1,128]{2,1,0:T(1,128)}), f32[8,1,128]{2,1,0:T(1,128)S(1)}, u32[]{:S(2)}, u32[]{:S(2)}) async-start(f32[8,1,128]{2,1,0:T(1,128)} %broadcast_in_dim.12), calls=%async_computation | async-start | bytes 8192 | tf_op jit(solution)/shard_map/all_to_all | solution.py:283
  7.0 0.0 copy-start.1
  7.0 1.6 %copy-done.1 = bf16[1,128,8192]{2,1,0:T(8,128)(2,1)S(1)} copy-done((bf16[1,128,8192]{2,1,0:T(8,128)(2,1)S(1)}, bf16[1,128,8192]{2,1,0:T(8,128)(2,1)}, u32[]{:S(2)}) %copy-start.1) | copy-done | bytes 2097176
  8.6 0.0 copy-start.2
  8.6 0.8 copy-done.2
  9.3 0.0 copy-start.3
  9.3 8.1 %gather.1.raw_ref = bf16[64,128,128]{2,1,0:T(8,128)(2,1)S(1)} custom-call(s32[64,128]{1,0:T(8,128)S(1)} %bitcast.9, bf16[128,8192]{1,0:T(8,128)(2,1)S(1)} %bitcast.8), custom_call_target="tpu_custom_call" | custom-call | bytes 25165824 | tf_op jit(solution)/shard_map/gather/pallas_call | solution.py:84
  17.4 0.0 all-to-all-done
  17.5 0.0 copy-done.5
  17.5 0.0 copy-done.3
  17.5 1.8 %fold.1 = bf16[64,136,128]{2,1,0:T(8,128)(2,1)} custom-call(bf16[64,128,128]{2,1,0:T(8,128)(2,1)S(1)} %gather.1.raw_ref, f32[8,128]{1,0:T(8,128)S(1)} %bitcast.10, f32[1,128]{1,0:T(1,128)S(1)} %copy-done.5, f32[64,128]{1,0:T(8,128)S(1)} %copy-done.3), custom_call_target="tpu_custom_call" | custom-call | bytes 5242880 | tf_op jit(solution)/shard_map/fold/pallas_call | solution.py:146
  19.3 0.0 copy-start.6
  19.3 16.2 %all-to-all-start.1 = ((bf16[64,136,128]{2,1,0:T(8,128)(2,1)}), bf16[64,136,128]{2,1,0:T(8,128)(2,1)S(1)}, u32[]{:S(2)}, u32[]{:S(2)}) async-start(bf16[64,136,128]{2,1,0:T(8,128)(2,1)} %fold.1), calls=%async_computation.1 | async-start | bytes 4456448 | tf_op jit(solution)/shard_map/all_to_all | solution.py:289
  35.5 0.0 copy-done.6
  35.6 1.0 copy.11.seeds_ref
  36.6 0.0 copy-start.4
  36.6 24.4 %probes.1.probes_ref = bf16[1024,8192]{1,0:T(8,128)(2,1)} custom-call(s32[4]{0:T(128)} %layer_ref.3, s32[1024,1]{1,0:T(8,128)} %copy.11.seeds_ref), custom_call_target="tpu_custom_call" | custom-call | bytes 67108864 | tf_op jit(solution)/shard_map/probes/pallas_call | solution.py:196
  60.9 34.1 %all-to-all-done.1.in_ref = bf16[64,136,128]{2,1,0:T(8,128)(2,1)S(1)} async-done(((bf16[64,136,128]{2,1,0:T(8,128)(2,1)}), bf16[64,136,128]{2,1,0:T(8,128)(2,1)S(1)}, u32[]{:S(2)}, u32[]{:S(2)}) %all-to-all-start.1) | async-done | bytes 2228256 | tf_op jit(solution)/shard_map/all_to_all | solution.py:289
  95.1 0.0 copy-done.4
  95.1 0.0 copy-start
  95.1 5.8 %copy-done = bf16[1024,8192]{1,0:T(8,128)(2,1)S(1)} copy-done((bf16[1024,8192]{1,0:T(8,128)(2,1)S(1)}, bf16[1024,8192]{1,0:T(8,128)(2,1)}, u32[]{:S(2)}) %copy-start) | copy-done | bytes 16777240
  100.8 7.1 %sketch.1 = (bf16[64,128,128]{2,1,0:T(8,128)(2,1)}, f32[1024,128]{1,0:T(8,128)}, f32[1,1024]{1,0:T(1,128)}, f32[64,128]{1,0:T(8,128)}) custom-call(s32[4]{0:T(128)S(1)} %copy-done.4, bf16[64,136,128]{2,1,0:T(8,128)(2,1)S(1)} %all-to-all-done.1.in_ref, bf16[1024,8192]{1,0:T(8,128)(2,1)S(1)} %copy-done), custom_call_target="tpu_custom_call" | custom-call | flops 2147483648 | bytes 23068672 | tf_op jit(solution)/shard_map/sketch/pallas_call | solution.py:259
Async XLA Ops:
  0.6 16.8 %copy-start.5 = (f32[1,128]{1,0:T(1,128)S(1)}, f32[1,128]{1,0:T(1,128)}, u32[]{:S(2)}) copy-start(f32[1,128]{1,0:T(1,128)} %own_ref.1) | copy-start | bytes 1540
  2.0 15.5 %all-to-all-start = ((f32[8,1,128]{2,1,0:T(1,128)}), f32[8,1,128]{2,1,0:T(1,128)S(1)}, u32[]{:S(2)}, u32[]{:S(2)}) async-start(f32[8,1,128]{2,1,0:T(1,128)} %broadcast_in_dim.12), calls=%async_computation | async-start | bytes 8192 | tf_op jit(solution)/shard_map/all_to_all | solution.py:283
  7.0 1.6 %copy-start.1 = (bf16[1,128,8192]{2,1,0:T(8,128)(2,1)S(1)}, bf16[1,128,8192]{2,1,0:T(8,128)(2,1)}, u32[]{:S(2)}) copy-start(bf16[1,128,8192]{2,1,0:T(8,128)(2,1)} %param.6) | copy-start | bytes 6291460
  8.6 0.8 copy-start.2
  9.3 8.1 %copy-start.3 = (f32[64,128]{1,0:T(8,128)S(1)}, f32[64,128]{1,0:T(8,128)}, u32[]{:S(2)}) copy-start(f32[64,128]{1,0:T(8,128)} %constant.2.clone.probe_ref) | copy-start | bytes 98308
  19.3 16.2 %copy-start.6 = (s32[1024]{0:T(1024)S(1)}, s32[1024]{0:T(1024)}, u32[]{:S(2)}) copy-start(s32[1024]{0:T(1024)} %param.10) | copy-start | bytes 12292
  19.3 75.7 %all-to-all-start.1 = ((bf16[64,136,128]{2,1,0:T(8,128)(2,1)}), bf16[64,136,128]{2,1,0:T(8,128)(2,1)S(1)}, u32[]{:S(2)}, u32[]{:S(2)}) async-start(bf16[64,136,128]{2,1,0:T(8,128)(2,1)} %fold.1), calls=%async_computation.1 | async-start | bytes 4456448 | tf_op jit(solution)/shard_map/all_to_all | solution.py:289
  36.6 58.5 %copy-start.4 = (s32[4]{0:T(128)S(1)}, s32[4]{0:T(128)}, u32[]{:S(2)}) copy-start(s32[4]{0:T(128)} %layer_ref.3) | copy-start | bytes 52
  95.1 5.8 %copy-start = (bf16[1024,8192]{1,0:T(8,128)(2,1)S(1)}, bf16[1024,8192]{1,0:T(8,128)(2,1)}, u32[]{:S(2)}) copy-start(bf16[1024,8192]{1,0:T(8,128)(2,1)} %probes.1.probes_ref) | copy-start | bytes 50331652

commit v4 on v3

--- a/solution.py
+++ b/solution.py
@@ -30,22 +30,17 @@
     return ((hashed % 511 - 255) / 256.0).astype(np.float32).reshape(GROUPS, COLS)
 
 
-def gather_kernel(order_ref, w_ref, out_ref, order, packed, pairs, turned, held, sem, out_sem):
+def gather_kernel(packed_ref, w_ref, out_ref, pairs, turned, held, sem, out_sem):
     half = GROUPS // 2
-    fetch = pltpu.make_async_copy(order_ref, order, sem.at[0])
-    fetch.start()
+    copy = pltpu.make_async_copy(packed_ref, pairs, sem)
+    copy.start()
 
     def turn(s, _):
         at = pl.multiple_of(s * 128, 128)
         turned[pl.ds(at, 128), :] = w_ref[:, pl.ds(at, 128)].T.astype(jnp.float32)
         return 0
 
-    lax.fori_loop(0, FF // 256, turn, 0, unroll=16)
-    fetch.wait()
-    packed[...] = order[0:half, :] + order[half:, :] * 65536
-    copy = pltpu.make_async_copy(packed, pairs, sem.at[1])
-    copy.start()
-    lax.fori_loop(FF // 256, FF // 128, turn, 0, unroll=16)
+    lax.fori_loop(0, FF // 128, turn, 0, unroll=16)
     copy.wait()
     sublane = lax.broadcasted_iota(jnp.int32, (8, 128), 0)
     masks = [sublane == i for i in range(8)]
@@ -81,24 +76,24 @@
 
 
 def gather(order, weights):
+    order = order.reshape(2, GROUPS // 2, COLS)
+    packed = order[0] + order[1] * 65536
     return pl.pallas_call(
         gather_kernel,
         out_shape=jax.ShapeDtypeStruct((GROUPS, ROWS, COLS), jnp.bfloat16),
-        in_specs=[ANY, VMEM],
+        in_specs=[VMEM, VMEM],
         out_specs=ANY,
         scratch_shapes=[
-            pltpu.VMEM((GROUPS, COLS), jnp.int32),
-            pltpu.VMEM((GROUPS // 2, COLS), jnp.int32),
             pltpu.SMEM((GROUPS // 2, COLS), jnp.int32),
             pltpu.VMEM((FF, ROWS), jnp.float32),
             pltpu.VMEM((GROUPS, ROWS, COLS), jnp.bfloat16),
-            pltpu.SemaphoreType.DMA((2,)),
+            pltpu.SemaphoreType.DMA,
             pltpu.SemaphoreType.DMA,
         ],
         compiler_params=pltpu.CompilerParams(vmem_limit_bytes=12 * MIB),
         cost_estimate=pl.CostEstimate(flops=0, bytes_accessed=24 * MIB, transcendentals=0),
         name="gather",
-    )(order.reshape(GROUPS, COLS), weights)
+    )(packed, weights)
 
 
 def pieces(value):

time: 108 us -> 108 us (level)
    unnamed x14 -> x12, local copies, waits for them, and re-layouts: 8.13 us -> 7.38 us
  transfers between devices with their start and end apart: 2 -> 2, of which waited for: 1 -> 1; matrix products, arithmetic and copies ran while one was open for 1% -> 2% of each run, Pallas kernels for 30% -> 30%
where the time goes in v4:
time: 108 us
  Pallas kernels  41 us (38%)
  waiting for transfers between devices  34.1 us (32%)
  starting transfers between devices  21.2 us (20%)
  local copies, waits for them, and re-layouts  9.72 us (9%)
    all_to_all x1, waiting for transfers between devices, local(): arrived = lax.all_to_all(blocks, STACK, 0, 0, tiled=True)  34.1 us
    pallas_call x1, Pallas kernels, make_probes(): pl.pallas_call(probes_kernel, out_shape=jax.ShapeDtypeStruct((PROBES, LAY...  24.4 us
    all_to_all x1, starting transfers between devices, local(): arrived = lax.all_to_all(blocks, STACK, 0, 0, tiled=True)  16.2 us
    pallas_call x1, Pallas kernels, gather(): pl.pallas_call(gather_kernel, out_shape=jax.ShapeDtypeStruct((GROUPS, ROW...  7.67 us
    unnamed x12, local copies, waits for them, and re-layouts  7.38 us
    pallas_call x1, Pallas kernels, sketch(): pl.pallas_call(sketch_kernel, out_shape=(jax.ShapeDtypeStruct((GROUPS, RO...  7.11 us
    all_to_all x1, starting transfers between devices, local(): lax.all_to_all(jnp.broadcast_to(branch_gains[None], (8, 1, ROWS)), 'exper...  5.03 us
  transfers between devices with their start and end apart: 2, of which 1 were waited for; matrix products, arithmetic and copies ran while one was open for 2% of the time, Pallas kernels for 30%

profile of v4, /device:TPU:17, one launch (start us, length us, event | category | flops | bytes accessed | tf_op | source)
XLA Modules:
  0.0 107.6 jit_solution(11364091521437555698)
XLA Ops:
  0.6 0.0 copy-start.2
  0.6 0.0 copy-start.4
  0.7 1.3 %broadcast_in_dim.12 = f32[8,1,128]{2,1,0:T(1,128)} broadcast(f32[128]{0:T(128)} %bitcast.11), dimensions={2} | broadcast | bytes 4608 | tf_op jit(solution)/shard_map/broadcast_in_dim | solution.py:279
  2.0 5.0 %all-to-all-start = ((f32[8,1,128]{2,1,0:T(1,128)}), f32[8,1,128]{2,1,0:T(1,128)S(1)}, u32[]{:S(2)}, u32[]{:S(2)}) async-start(f32[8,1,128]{2,1,0:T(1,128)} %broadcast_in_dim.12), calls=%async_computation | async-start | bytes 8192 | tf_op jit(solution)/shard_map/all_to_all | solution.py:278
  7.0 0.8 multiply_add_fusion
  7.8 0.0 copy-start.1
  7.8 1.6 %copy-done.1 = bf16[1,128,8192]{2,1,0:T(8,128)(2,1)S(1)} copy-done((bf16[1,128,8192]{2,1,0:T(8,128)(2,1)S(1)}, bf16[1,128,8192]{2,1,0:T(8,128)(2,1)}, u32[]{:S(2)}) %copy-start.1) | copy-done | bytes 2097176
  9.4 7.7 %gather.1.raw_ref = bf16[64,128,128]{2,1,0:T(8,128)(2,1)S(1)} custom-call(s32[32,128]{1,0:T(8,128)S(1)} %bitcast.9, bf16[128,8192]{1,0:T(8,128)(2,1)S(1)} %bitcast.8), custom_call_target="tpu_custom_call" | custom-call | bytes 25165824 | tf_op jit(solution)/shard_map/gather/pallas_call | solution.py:81
  17.0 0.0 all-to-all-done
  17.1 0.0 copy-done.2
  17.1 0.0 copy-done.4
  17.1 1.8 %fold.1 = bf16[64,136,128]{2,1,0:T(8,128)(2,1)} custom-call(bf16[64,128,128]{2,1,0:T(8,128)(2,1)S(1)} %gather.1.raw_ref, f32[8,128]{1,0:T(8,128)S(1)} %bitcast.10, f32[1,128]{1,0:T(1,128)S(1)} %copy-done.4, f32[64,128]{1,0:T(8,128)S(1)} %copy-done.2), custom_call_target="tpu_custom_call" | custom-call | bytes 5242880 | tf_op jit(solution)/shard_map/fold/pallas_call | solution.py:141
  18.9 0.0 copy-start.5
  18.9 16.2 %all-to-all-start.1 = ((bf16[64,136,128]{2,1,0:T(8,128)(2,1)}), bf16[64,136,128]{2,1,0:T(8,128)(2,1)S(1)}, u32[]{:S(2)}, u32[]{:S(2)}) async-start(bf16[64,136,128]{2,1,0:T(8,128)(2,1)} %fold.1), calls=%async_computation.1 | async-start | bytes 4456448 | tf_op jit(solution)/shard_map/all_to_all | solution.py:284
  35.1 0.0 copy-done.5
  35.2 1.0 copy.11.seeds_ref
  36.2 0.0 copy-start.3
  36.2 24.4 %probes.1.probes_ref = bf16[1024,8192]{1,0:T(8,128)(2,1)} custom-call(s32[4]{0:T(128)} %layer_ref.3, s32[1024,1]{1,0:T(8,128)} %copy.11.seeds_ref), custom_call_target="tpu_custom_call" | custom-call | bytes 67108864 | tf_op jit(solution)/shard_map/probes/pallas_call | solution.py:191
  60.5 34.1 %all-to-all-done.1.in_ref = bf16[64,136,128]{2,1,0:T(8,128)(2,1)S(1)} async-done(((bf16[64,136,128]{2,1,0:T(8,128)(2,1)}), bf16[64,136,128]{2,1,0:T(8,128)(2,1)S(1)}, u32[]{:S(2)}, u32[]{:S(2)}) %all-to-all-start.1) | async-done | bytes 2228256 | tf_op jit(solution)/shard_map/all_to_all | solution.py:284
  94.7 0.0 copy-done.3
  94.7 0.0 copy-start
  94.7 5.8 %copy-done = bf16[1024,8192]{1,0:T(8,128)(2,1)S(1)} copy-done((bf16[1024,8192]{1,0:T(8,128)(2,1)S(1)}, bf16[1024,8192]{1,0:T(8,128)(2,1)}, u32[]{:S(2)}) %copy-start) | copy-done | bytes 16777240
  100.5 7.1 %sketch.1 = (bf16[64,128,128]{2,1,0:T(8,128)(2,1)}, f32[1024,128]{1,0:T(8,128)}, f32[1,1024]{1,0:T(1,128)}, f32[64,128]{1,0:T(8,128)}) custom-call(s32[4]{0:T(128)S(1)} %copy-done.3, bf16[64,136,128]{2,1,0:T(8,128)(2,1)S(1)} %all-to-all-done.1.in_ref, bf16[1024,8192]{1,0:T(8,128)(2,1)S(1)} %copy-done), custom_call_target="tpu_custom_call" | custom-call | flops 2147483648 | bytes 23068672 | tf_op jit(solution)/shard_map/sketch/pallas_call | solution.py:254
Async XLA Ops:
  0.6 16.4 %copy-start.2 = (f32[64,128]{1,0:T(8,128)S(1)}, f32[64,128]{1,0:T(8,128)}, u32[]{:S(2)}) copy-start(f32[64,128]{1,0:T(8,128)} %constant.4.clone.probe_ref) | copy-start | bytes 98308
  0.6 16.4 %copy-start.4 = (f32[1,128]{1,0:T(1,128)S(1)}, f32[1,128]{1,0:T(1,128)}, u32[]{:S(2)}) copy-start(f32[1,128]{1,0:T(1,128)} %own_ref.1) | copy-start | bytes 1540
  2.0 15.1 %all-to-all-start = ((f32[8,1,128]{2,1,0:T(1,128)}), f32[8,1,128]{2,1,0:T(1,128)S(1)}, u32[]{:S(2)}, u32[]{:S(2)}) async-start(f32[8,1,128]{2,1,0:T(1,128)} %broadcast_in_dim.12), calls=%async_computation | async-start | bytes 8192 | tf_op jit(solution)/shard_map/all_to_all | solution.py:278
  7.8 1.6 %copy-start.1 = (bf16[1,128,8192]{2,1,0:T(8,128)(2,1)S(1)}, bf16[1,128,8192]{2,1,0:T(8,128)(2,1)}, u32[]{:S(2)}) copy-start(bf16[1,128,8192]{2,1,0:T(8,128)(2,1)} %param.6) | copy-start | bytes 6291460
  18.9 16.2 %copy-start.5 = (s32[1024]{0:T(1024)S(1)}, s32[1024]{0:T(1024)}, u32[]{:S(2)}) copy-start(s32[1024]{0:T(1024)} %param.10) | copy-start | bytes 12292
  18.9 75.7 %all-to-all-start.1 = ((bf16[64,136,128]{2,1,0:T(8,128)(2,1)}), bf16[64,136,128]{2,1,0:T(8,128)(2,1)S(1)}, u32[]{:S(2)}, u32[]{:S(2)}) async-start(bf16[64,136,128]{2,1,0:T(8,128)(2,1)} %fold.1), calls=%async_computation.1 | async-start | bytes 4456448 | tf_op jit(solution)/shard_map/all_to_all | solution.py:284
  36.2 58.5 %copy-start.3 = (s32[4]{0:T(128)S(1)}, s32[4]{0:T(128)}, u32[]{:S(2)}) copy-start(s32[4]{0:T(128)} %layer_ref.3) | copy-start | bytes 52
  94.7 5.8 %copy-start = (bf16[1024,8192]{1,0:T(8,128)(2,1)S(1)}, bf16[1024,8192]{1,0:T(8,128)(2,1)}, u32[]{:S(2)}) copy-start(bf16[1024,8192]{1,0:T(8,128)(2,1)} %probes.1.probes_ref) | copy-start | bytes 50331652

commit v5 on v4

--- a/solution.py
+++ b/solution.py
@@ -30,7 +30,7 @@
     return ((hashed % 511 - 255) / 256.0).astype(np.float32).reshape(GROUPS, COLS)
 
 
-def gather_kernel(packed_ref, w_ref, out_ref, pairs, turned, held, sem, out_sem):
+def gather_kernel(packed_ref, w_ref, out_ref, pairs, turned, sem):
     half = GROUPS // 2
     copy = pltpu.make_async_copy(packed_ref, pairs, sem)
     copy.start()
@@ -44,11 +44,6 @@
     copy.wait()
     sublane = lax.broadcasted_iota(jnp.int32, (8, 128), 0)
     masks = [sublane == i for i in range(8)]
-
-    def send(at, count):
-        return pltpu.make_async_copy(
-            held.at[pl.ds(at, count)], out_ref.at[pl.ds(at, count)], out_sem
-        )
 
     def both(p):
         tiles = ([], [])
@@ -62,17 +57,14 @@
             for u in range(2):
                 tiles[u].append(made[u])
         for u in range(2):
-            held[p + half * u] = jnp.concatenate(tiles[u], axis=0).astype(jnp.bfloat16).T
+            out_ref[p + half * u] = jnp.concatenate(tiles[u], axis=0).astype(jnp.bfloat16).T
 
     def step(s, _):
         for q in range(8):
             both(s * 8 + q)
-        send(s * 8, 8).start()
-        send(s * 8 + half, 8).start()
         return 0
 
     lax.fori_loop(0, half // 8, step, 0)
-    send(0, GROUPS).wait()
 
 
 def gather(order, weights):
@@ -82,12 +74,10 @@
         gather_kernel,
         out_shape=jax.ShapeDtypeStruct((GROUPS, ROWS, COLS), jnp.bfloat16),
         in_specs=[VMEM, VMEM],
-        out_specs=ANY,
+        out_specs=VMEM,
         scratch_shapes=[
             pltpu.SMEM((GROUPS // 2, COLS), jnp.int32),
             pltpu.VMEM((FF, ROWS), jnp.float32),
-            pltpu.VMEM((GROUPS, ROWS, COLS), jnp.bfloat16),
-            pltpu.SemaphoreType.DMA,
             pltpu.SemaphoreType.DMA,
         ],
         compiler_params=pltpu.CompilerParams(vmem_limit_bytes=12 * MIB),

time: 108 us -> 108 us (level)
  no operation moved by 1% of the time
where the time goes in v5:
time: 108 us; the launch traced here: 107 us
  Pallas kernels  40.8 us (38%)
  waiting for transfers between devices  34.1 us (32%)
  starting transfers between devices  21.2 us (20%)
  local copies, waits for them, and re-layouts  9.72 us (9%)
    all_to_all x1, waiting for transfers between devices, local(): arrived = lax.all_to_all(blocks, STACK, 0, 0, tiled=True)  34.1 us
    pallas_call x1, Pallas kernels, make_probes(): pl.pallas_call(probes_kernel, out_shape=jax.ShapeDtypeStruct((PROBES, LAY...  24.4 us
    all_to_all x1, starting transfers between devices, local(): arrived = lax.all_to_all(blocks, STACK, 0, 0, tiled=True)  16.2 us
    pallas_call x1, Pallas kernels, gather(): pl.pallas_call(gather_kernel, out_shape=jax.ShapeDtypeStruct((GROUPS, ROW...  7.5 us
    unnamed x12, local copies, waits for them, and re-layouts  7.38 us
    pallas_call x1, Pallas kernels, sketch(): pl.pallas_call(sketch_kernel, out_shape=(jax.ShapeDtypeStruct((GROUPS, RO...  7.11 us
    all_to_all x1, starting transfers between devices, local(): lax.all_to_all(jnp.broadcast_to(branch_gains[None], (8, 1, ROWS)), 'exper...  5.03 us
  transfers between devices with their start and end apart: 2, of which 1 were waited for; matrix products, arithmetic and copies ran while one was open for 2% of the time, Pallas kernels for 30%

profile of v5, /device:TPU:17, one launch (start us, length us, event | category | flops | bytes accessed | tf_op | source)
XLA Modules:
  0.0 107.4 jit_solution(10618081701999127768)
XLA Ops:
  0.6 0.0 copy-start.2
  0.6 0.0 copy-start.4
  0.7 1.3 %broadcast_in_dim.12 = f32[8,1,128]{2,1,0:T(1,128)} broadcast(f32[128]{0:T(128)} %bitcast.11), dimensions={2} | broadcast | bytes 4608 | tf_op jit(solution)/shard_map/broadcast_in_dim | solution.py:269
  2.0 5.0 %all-to-all-start = ((f32[8,1,128]{2,1,0:T(1,128)}), f32[8,1,128]{2,1,0:T(1,128)S(1)}, u32[]{:S(2)}, u32[]{:S(2)}) async-start(f32[8,1,128]{2,1,0:T(1,128)} %broadcast_in_dim.12), calls=%async_computation | async-start | bytes 8192 | tf_op jit(solution)/shard_map/all_to_all | solution.py:268
  7.0 0.8 multiply_add_fusion
  7.8 0.0 copy-start.1
  7.8 1.6 %copy-done.1 = bf16[1,128,8192]{2,1,0:T(8,128)(2,1)S(1)} copy-done((bf16[1,128,8192]{2,1,0:T(8,128)(2,1)S(1)}, bf16[1,128,8192]{2,1,0:T(8,128)(2,1)}, u32[]{:S(2)}) %copy-start.1) | copy-done | bytes 2097176
  9.4 7.5 %gather.1.raw_ref = bf16[64,128,128]{2,1,0:T(8,128)(2,1)S(1)} custom-call(s32[32,128]{1,0:T(8,128)S(1)} %bitcast.9, bf16[128,8192]{1,0:T(8,128)(2,1)S(1)} %bitcast.8), custom_call_target="tpu_custom_call" | custom-call | bytes 25165824 | tf_op jit(solution)/shard_map/gather/pallas_call | solution.py:73
  16.9 0.0 all-to-all-done
  16.9 0.0 copy-done.2
  16.9 0.0 copy-done.4
  16.9 1.8 %fold.1 = bf16[64,136,128]{2,1,0:T(8,128)(2,1)} custom-call(bf16[64,128,128]{2,1,0:T(8,128)(2,1)S(1)} %gather.1.raw_ref, f32[8,128]{1,0:T(8,128)S(1)} %bitcast.10, f32[1,128]{1,0:T(1,128)S(1)} %copy-done.4, f32[64,128]{1,0:T(8,128)S(1)} %copy-done.2), custom_call_target="tpu_custom_call" | custom-call | bytes 5242880 | tf_op jit(solution)/shard_map/fold/pallas_call | solution.py:131
  18.8 0.0 copy-start.5
  18.8 16.2 %all-to-all-start.1 = ((bf16[64,136,128]{2,1,0:T(8,128)(2,1)}), bf16[64,136,128]{2,1,0:T(8,128)(2,1)S(1)}, u32[]{:S(2)}, u32[]{:S(2)}) async-start(bf16[64,136,128]{2,1,0:T(8,128)(2,1)} %fold.1), calls=%async_computation.1 | async-start | bytes 4456448 | tf_op jit(solution)/shard_map/all_to_all | solution.py:274
  35.0 0.0 copy-done.5
  35.0 1.0 copy.11.seeds_ref
  36.0 0.0 copy-start.3
  36.0 24.4 %probes.1.probes_ref = bf16[1024,8192]{1,0:T(8,128)(2,1)} custom-call(s32[4]{0:T(128)} %layer_ref.3, s32[1024,1]{1,0:T(8,128)} %copy.11.seeds_ref), custom_call_target="tpu_custom_call" | custom-call | bytes 67108864 | tf_op jit(solution)/shard_map/probes/pallas_call | solution.py:181
  60.4 34.1 %all-to-all-done.1.in_ref = bf16[64,136,128]{2,1,0:T(8,128)(2,1)S(1)} async-done(((bf16[64,136,128]{2,1,0:T(8,128)(2,1)}), bf16[64,136,128]{2,1,0:T(8,128)(2,1)S(1)}, u32[]{:S(2)}, u32[]{:S(2)}) %all-to-all-start.1) | async-done | bytes 2228256 | tf_op jit(solution)/shard_map/all_to_all | solution.py:274
  94.5 0.0 copy-done.3
  94.5 0.0 copy-start
  94.5 5.8 %copy-done = bf16[1024,8192]{1,0:T(8,128)(2,1)S(1)} copy-done((bf16[1024,8192]{1,0:T(8,128)(2,1)S(1)}, bf16[1024,8192]{1,0:T(8,128)(2,1)}, u32[]{:S(2)}) %copy-start) | copy-done | bytes 16777240
  100.3 7.1 %sketch.1 = (bf16[64,128,128]{2,1,0:T(8,128)(2,1)}, f32[1024,128]{1,0:T(8,128)}, f32[1,1024]{1,0:T(1,128)}, f32[64,128]{1,0:T(8,128)}) custom-call(s32[4]{0:T(128)S(1)} %copy-done.3, bf16[64,136,128]{2,1,0:T(8,128)(2,1)S(1)} %all-to-all-done.1.in_ref, bf16[1024,8192]{1,0:T(8,128)(2,1)S(1)} %copy-done), custom_call_target="tpu_custom_call" | custom-call | flops 2147483648 | bytes 23068672 | tf_op jit(solution)/shard_map/sketch/pallas_call | solution.py:244
Async XLA Ops:
  0.6 16.2 %copy-start.2 = (f32[64,128]{1,0:T(8,128)S(1)}, f32[64,128]{1,0:T(8,128)}, u32[]{:S(2)}) copy-start(f32[64,128]{1,0:T(8,128)} %constant.4.clone.probe_ref) | copy-start | bytes 98308
  0.6 16.2 %copy-start.4 = (f32[1,128]{1,0:T(1,128)S(1)}, f32[1,128]{1,0:T(1,128)}, u32[]{:S(2)}) copy-start(f32[1,128]{1,0:T(1,128)} %own_ref.1) | copy-start | bytes 1540
  2.0 14.9 %all-to-all-start = ((f32[8,1,128]{2,1,0:T(1,128)}), f32[8,1,128]{2,1,0:T(1,128)S(1)}, u32[]{:S(2)}, u32[]{:S(2)}) async-start(f32[8,1,128]{2,1,0:T(1,128)} %broadcast_in_dim.12), calls=%async_computation | async-start | bytes 8192 | tf_op jit(solution)/shard_map/all_to_all | solution.py:268
  7.8 1.6 %copy-start.1 = (bf16[1,128,8192]{2,1,0:T(8,128)(2,1)S(1)}, bf16[1,128,8192]{2,1,0:T(8,128)(2,1)}, u32[]{:S(2)}) copy-start(bf16[1,128,8192]{2,1,0:T(8,128)(2,1)} %param.6) | copy-start | bytes 6291460
  18.8 16.2 %copy-start.5 = (s32[1024]{0:T(1024)S(1)}, s32[1024]{0:T(1024)}, u32[]{:S(2)}) copy-start(s32[1024]{0:T(1024)} %param.10) | copy-start | bytes 12292
  18.8 75.7 %all-to-all-start.1 = ((bf16[64,136,128]{2,1,0:T(8,128)(2,1)}), bf16[64,136,128]{2,1,0:T(8,128)(2,1)S(1)}, u32[]{:S(2)}, u32[]{:S(2)}) async-start(bf16[64,136,128]{2,1,0:T(8,128)(2,1)} %fold.1), calls=%async_computation.1 | async-start | bytes 4456448 | tf_op jit(solution)/shard_map/all_to_all | solution.py:274
  36.0 58.5 %copy-start.3 = (s32[4]{0:T(128)S(1)}, s32[4]{0:T(128)}, u32[]{:S(2)}) copy-start(s32[4]{0:T(128)} %layer_ref.3) | copy-start | bytes 52
  94.5 5.8 %copy-start = (bf16[1024,8192]{1,0:T(8,128)(2,1)S(1)}, bf16[1024,8192]{1,0:T(8,128)(2,1)}, u32[]{:S(2)}) copy-start(bf16[1024,8192]{1,0:T(8,128)(2,1)} %probes.1.probes_ref) | copy-start | bytes 50331652
